TPU v7x, 32 devices: a whole 2x2x4 slice. The times are simulated.
32 devices in a mesh: dp: 2 (over x), expert: 16 (over z, y, core).
Axes of the slice: x: 2, y: 2, z: 4, core: 2. Of those that a mesh axis runs over, the one named last changes fastest.
Arguments:
- tokens: bfloat16 [4096, 1024], P(('dp', 'expert')), may hold values from -6 to 6
- route_ids: int32 [4096, 4], P(('dp', 'expert')), may hold values from 0 to 15, all different within a row; in each aligned block of 128 rows (0 to 127, 128 to 255, ...) at most 48 rows name the same one
- route_weights: float32 [4096, 4], P(('dp', 'expert')), may hold values from 0.2 to 1
- up_weight: bfloat16 [16, 1024, 704], P('expert', 'dp'), may hold values from -0.1875 to 0.1875
- down_weight: bfloat16 [16, 1024, 704], P('expert', 'dp'), may hold values from -0.21875 to 0.21875
- head_weight: bfloat16 [1024, 1024], P('dp'), may hold values from -0.75 to 0.75
- out_weight: float32 [1024], P('dp'), may hold values from -0.375 to 0.375
- pool_ids: int32 [32, 128], P(('dp', 'expert')), may hold values from 0 to 15, never falling along the last dimension, each value on 1 to 64 neighbouring positions
- list_ids: int32 [32, 16], P(('dp', 'expert')), may hold values from 0 to 7, as said below
- clicks: int32 [32, 16], P(('dp', 'expert')), may hold values 0 or 1
- ranks: int32 [32, 16], P(('dp', 'expert')), may hold values from 0 to 31
- alpha_table: float32 [32], replicated, may hold values from 0.3 to 1
- beta_table: float32 [32], replicated, may hold values from 0 to 0.3
Outputs:
- grad_up: bfloat16 [16, 1024, 704], P('expert', 'dp')
- grad_down: bfloat16 [16, 1024, 704], P('expert', 'dp')
- grad_head: float32 [1024, 1024], P('dp')
- grad_out: float32 [1024], P('dp')
- list_loss: float32 [16], P('expert')
Inputs may be any that keep to these rules, and one draw needn't show every extreme that they name: `route_ids`: each token names 4 different experts; among the 128 tokens of one device no expert is named more than 48 times, a bound that some block reaches. `pool_ids`: in each row the candidate number never falls, every candidate has 1 to 64 tokens and one has exactly 64. `list_ids`: every list number appears in every row.
All inputs are finite; a program needn't handle non-finite values. No bound on the sum of `clicks` on one device may be relied on, other than what follows from the above.
Results may differ from a plain program's by a relative error of at most 0.028.
Values may be sent and summed in bfloat16 or wider, within the bound.
No kernel may reach another device: no remote copies, remote signals or barrier semaphores. Data moves between devices by JAX's collectives and lax.ppermute only.
A program may use at most 64 MiB of HBM per device.

v0:
```python
import jax
import jax.numpy as jnp
import numpy as np
from jax import lax
from jax.experimental import pallas as pl
from jax.experimental.pallas import tpu as pltpu
from jax.sharding import PartitionSpec as P

LISTS = 8
RANKS = 32
BF = jnp.bfloat16
F32 = jnp.float32


def ring_order(chips):
    cols = 1
    while cols * cols * 4 <= chips and chips % (cols * 2) == 0:
        cols *= 2
    rows = chips // cols
    if cols == 1:
        return list(range(chips))
    cycle = [(r, 0) for r in range(rows)]
    for turn, r in enumerate(reversed(range(rows))):
        across = list(range(1, cols))
        if turn % 2:
            across.reverse()
        cycle += [(r, c) for c in across]
    return [r * cols + c for r, c in cycle]


class Ring:
    def __init__(self, devices):
        self.chips = devices // 2
        self.half = self.chips // 2
        cycle = ring_order(self.chips)
        count = self.chips
        self.forward = []
        for p in range(count):
            self.forward.append((2 * cycle[p], 2 * cycle[(p + 1) % count]))
            self.forward.append((2 * cycle[p] + 1, 2 * cycle[(p - 1) % count] + 1))
        self.swap_pairs = [(d, d ^ 1) for d in range(devices)]
        position = {chip: p for p, chip in enumerate(cycle)}
        table = np.zeros((devices, devices), np.int32)
        for device in range(devices):
            pos, core = position[device // 2], device % 2
            sign = 1 if core else -1

            def at(step, which):
                return 2 * cycle[(pos + step) % count] + which

            order = [at(0, core), at(0, 1 - core)]
            for r in range(1, self.half):
                order += [at(sign * r, core), at(sign * r, 1 - core)]
                order += [at(-sign * r, 1 - core), at(-sign * r, core)]
            order += [at(self.half, core), at(self.half, 1 - core)]
            table[device] = order
        self.table = table

    def send(self, x):
        return lax.ppermute(x, "expert", self.forward)

    def swap(self, x):
        return lax.ppermute(x, "expert", self.swap_pairs)

    def gather(self, x):
        rows = x.shape[0]
        partner = self.swap(x)
        current = jnp.concatenate([x, partner], axis=0)
        rounds = [[x, partner]]
        for r in range(1, self.half + 1):
            outgoing = current[:rows] if r == self.half else current
            current = self.send(outgoing)
            rounds.append([current, self.swap(current)])
        return rounds


def silu_slope(pre_act):
    sigmoid = jax.nn.sigmoid(pre_act)
    return sigmoid * (1.0 + pre_act * (1.0 - sigmoid))


def routed_local(
    tokens,
    route_ids,
    route_weights,
    up_weight,
    down_weight,
    head_weight,
    out_weight,
    pool_ids,
    list_ids,
    clicks,
    ranks,
    alpha_table,
    beta_table,
):
    tok_count = tokens.shape[0]
    model_width = tokens.shape[1]
    top_count = route_ids.shape[1]
    owners = lax.axis_size("expert")
    capacity = 3 * tok_count * top_count // (2 * owners)
    slot_total = owners * capacity
    flat_ids = route_ids.reshape(-1)
    expert_hot = (flat_ids[:, None] == jnp.arange(owners, dtype=jnp.int32)[None, :]).astype(
        jnp.int32
    )
    running = jnp.cumsum(expert_hot, axis=0) - 1
    slot_index = jnp.sum(running * expert_hot, axis=1)
    target = flat_ids * capacity + slot_index
    token_index = jnp.arange(tok_count * top_count, dtype=jnp.int32) // top_count
    outgoing = (
        jnp.zeros((slot_total, model_width), jnp.bfloat16).at[target].set(tokens[token_index])
    )
    received = lax.all_to_all(
        outgoing.reshape(owners, capacity, model_width),
        "expert",
        split_axis=0,
        concat_axis=0,
        tiled=True,
    )
    inputs = received.reshape(slot_total, model_width)
    up_local = up_weight[0]
    down_local = down_weight[0]
    hidden_width = up_local.shape[1]
    columns = inputs
    pre_act = jnp.dot(
        columns,
        lax.all_gather(up_local, "dp", axis=0, tiled=True),
        preferred_element_type=jnp.float32,
    )
    activated = jax.nn.silu(pre_act).astype(jnp.bfloat16)
    expert_out = lax.dot_general(
        activated,
        lax.all_gather(down_local, "dp", axis=0, tiled=True),
        (((1,), (1,)), ((), ())),
        preferred_element_type=jnp.float32,
    ).astype(jnp.bfloat16)
    returned = lax.all_to_all(
        expert_out.reshape(owners, capacity, model_width),
        "expert",
        split_axis=0,
        concat_axis=0,
        tiled=True,
    ).reshape(slot_total, model_width)
    routed_rows = returned[target].reshape(tok_count, top_count, model_width)
    routed = jnp.sum(route_weights[:, :, None] * routed_rows.astype(jnp.float32), axis=1)
    mixed = tokens.astype(jnp.float32) + routed
    inv_rms = lax.rsqrt(jnp.mean(mixed * mixed, axis=1, keepdims=True) + 1e-06)
    normed = mixed * inv_rms
    cand_count = list_ids.shape[1]
    member = (pool_ids[0][:, None] == jnp.arange(cand_count, dtype=jnp.int32)[None, :]).astype(
        jnp.float32
    )
    token_counts = jnp.sum(member, axis=0)
    pooled_sum = lax.dot_general(
        member,
        normed,
        (((0,), (0,)), ((), ())),
        precision=lax.Precision.HIGHEST,
        preferred_element_type=jnp.float32,
    )
    pooled = (pooled_sum / token_counts[:, None]).astype(jnp.bfloat16)
    all_pooled = lax.all_gather(pooled, "dp", axis=0, tiled=True)
    head_act = jnp.tanh(
        lax.dot_general(
            all_pooled, head_weight, (((1,), (1,)), ((), ())), preferred_element_type=jnp.float32
        )
    )
    part_score = jnp.sum(head_act * out_weight[None, :], axis=1)
    rank_hot = (ranks[0][:, None] == jnp.arange(RANKS, dtype=jnp.int32)[None, :]).astype(
        jnp.float32
    )
    alpha_of = jnp.sum(rank_hot * alpha_table[None, :], axis=1)
    beta_of = jnp.sum(rank_hot * beta_table[None, :], axis=1)
    corrected = (clicks[0].astype(jnp.float32) - beta_of) / alpha_of
    list_hot = (list_ids[0][:, None] == jnp.arange(LISTS, dtype=jnp.int32)[None, :]).astype(
        jnp.float32
    )
    group_corrected, group_lists = (
        lax.all_gather(corrected, "dp", axis=0, tiled=True),
        lax.all_gather(list_hot, "dp", axis=0, tiled=True),
    )
    group_scores = lax.psum(part_score, "dp")
    exp_scores = jnp.exp(group_scores)
    exp_total = jnp.sum(exp_scores[:, None] * group_lists, axis=0)
    click_total = jnp.sum(group_corrected[:, None] * group_lists, axis=0)
    cross_total = jnp.sum((group_corrected * group_scores)[:, None] * group_lists, axis=0)
    list_loss = jnp.sum(click_total * jnp.log(exp_total) - cross_total).reshape(1)
    group_grad = (
        jnp.sum(group_lists * (click_total / exp_total)[None, :], axis=1) * exp_scores
        - group_corrected
    )
    hid_grad = (group_grad[:, None] * out_weight[None, :] * (1.0 - head_act * head_act)).astype(
        jnp.bfloat16
    )
    head_term = lax.dot_general(
        hid_grad, all_pooled, (((0,), (0,)), ((), ())), preferred_element_type=jnp.float32
    )
    out_term = jnp.sum(group_grad[:, None] * head_act, axis=0)
    grad_head, grad_out = (
        lax.psum(head_term.astype(jnp.bfloat16), "expert").astype(jnp.float32),
        lax.psum(out_term.astype(jnp.bfloat16), "expert").astype(jnp.float32),
    )
    pooled_grad = lax.psum_scatter(
        jnp.dot(hid_grad, head_weight, preferred_element_type=jnp.float32).astype(jnp.bfloat16),
        "dp",
        scatter_dimension=0,
        tiled=True,
    ).astype(jnp.float32)
    normed_grad = jnp.dot(
        member,
        pooled_grad / token_counts[:, None],
        precision=lax.Precision.HIGHEST,
        preferred_element_type=jnp.float32,
    )
    mixed_grad = inv_rms * (
        normed_grad - normed * jnp.mean(normed_grad * normed, axis=1, keepdims=True)
    )
    cotangent = (
        (route_weights[:, :, None] * mixed_grad[:, None, :])
        .astype(jnp.bfloat16)
        .reshape(tok_count * top_count, model_width)
    )
    outgoing_grad = jnp.zeros((slot_total, model_width), jnp.bfloat16).at[target].set(cotangent)
    slot_grad = lax.all_to_all(
        outgoing_grad.reshape(owners, capacity, model_width),
        "expert",
        split_axis=0,
        concat_axis=0,
        tiled=True,
    ).reshape(slot_total, model_width)
    columns = slot_grad
    act_grad = jnp.dot(
        columns,
        lax.all_gather(down_local, "dp", axis=0, tiled=True),
        preferred_element_type=jnp.float32,
    )
    pre_grad = (act_grad * silu_slope(pre_act)).astype(jnp.bfloat16)
    up_term = lax.dot_general(
        inputs, pre_grad, (((0,), (0,)), ((), ())), preferred_element_type=jnp.float32
    )
    down_term = lax.dot_general(
        slot_grad, activated, (((0,), (0,)), ((), ())), preferred_element_type=jnp.float32
    )
    summed = lax.psum_scatter(
        jnp.concatenate([up_term, down_term], axis=1).astype(jnp.bfloat16),
        "dp",
        scatter_dimension=0,
        tiled=True,
    ).astype(jnp.float32)
    grad_up = summed[:, :hidden_width].astype(jnp.bfloat16)[None]
    grad_down = summed[:, hidden_width:].astype(jnp.bfloat16)[None]
    return (grad_up, grad_down, grad_head, grad_out, list_loss)


SPARE_VMEM = 6 * 1024 * 1024


def padded_bytes(x):
    lead = int(np.prod(x.shape[:-2])) if len(x.shape) > 2 else 1
    rows = -(-x.shape[-2] // 16) * 16 if len(x.shape) > 1 else 1
    return lead * rows * (-(-x.shape[-1] // 128) * 128) * x.dtype.itemsize


def vmem_call(kernel, outs, args, scratch=(), flops=0, smem=0):
    held = sum(padded_bytes(a) for a in list(args)[smem:] + list(outs))
    held += sum(int(np.prod(b.shape)) * jnp.dtype(b.dtype).itemsize for b in scratch)
    specs = [pl.BlockSpec(memory_space=pltpu.SMEM)] * smem + [
        pl.BlockSpec(memory_space=pltpu.VMEM)
    ] * (len(args) - smem)
    moved = sum(a.size * a.dtype.itemsize for a in args) + sum(
        o.size * o.dtype.itemsize for o in outs
    )
    return pl.pallas_call(
        kernel,
        out_shape=outs,
        in_specs=specs,
        out_specs=[pl.BlockSpec(memory_space=pltpu.VMEM)] * len(outs),
        scratch_shapes=list(scratch),
        cost_estimate=pl.CostEstimate(flops=flops, bytes_accessed=moved, transcendentals=0),
        compiler_params=pltpu.CompilerParams(vmem_limit_bytes=held + SPARE_VMEM),
    )(*args)


def shaped(shape, dtype):
    return jax.ShapeDtypeStruct(shape, dtype)


def fill(buffer, refs, start=0, limit=None):
    at = 0
    for ref in refs:
        size = limit or ref.shape[0]
        buffer[pl.ds(at, size), :] = ref[:size, start : start + buffer.shape[1]]
        at += size


def dot_rows(a, b):
    return lax.dot_general(a, b, (((1,), (1,)), ((), ())), preferred_element_type=F32)


def pack_stage(tokens, ids, weights, owners):
    tok, width = tokens.shape
    half = width // 2
    per_row = width // tok
    top = ids.shape[0]
    extra = 2 * -(-owners // per_row)
    rows = tok + -(-extra // 8) * 8

    def kernel(tok_ref, id_ref, weight_ref, out_ref):
        swapped = lax.axis_index("dp") != 0
        out_ref[:tok, :half] = jnp.where(swapped, tok_ref[:, half:], tok_ref[:, :half])
        out_ref[:tok, half:] = jnp.where(swapped, tok_ref[:, :half], tok_ref[:, half:])
        lanes = [[] for _ in range(extra)]
        for owner in range(owners):
            value = jnp.zeros((1, tok), F32)
            for k in range(top):
                hit = id_ref[k : k + 1, :] == owner
                value = value + jnp.where(hit, weight_ref[k : k + 1, :], 0.0)
            high = value.astype(BF).astype(F32)
            row = owner // per_row
            lanes[2 * row].append(high)
            lanes[2 * row + 1].append(value - high)
        filled = []
        for row in lanes:
            row += [jnp.zeros((1, tok), F32)] * (per_row - len(row))
            filled.append(jnp.concatenate(row, axis=1))
        filled.append(jnp.zeros((rows - tok - extra, width), F32))
        out_ref[tok:, :] = jnp.concatenate(filled, axis=0).astype(BF)

    return vmem_call(kernel, [shaped((rows, width), BF)], [tokens, ids, weights])[0]


def weight_column(ref, tok, owners, mine):
    width = ref.shape[1]
    per_row = width // tok
    extra = ref[tok:, :].astype(F32)
    row = jnp.zeros((1, tok), F32)
    for owner in range(owners):
        at, lane = 2 * (owner // per_row), (owner % per_row) * tok
        both = extra[at : at + 1, lane : lane + tok] + extra[at + 1 : at + 2, lane : lane + tok]
        row = row + jnp.where(mine == owner, both, 0.0)
    diagonal = lax.broadcasted_iota(jnp.int32, (tok, tok), 0) == lax.broadcasted_iota(
        jnp.int32, (tok, tok), 1
    )
    return jnp.sum(jnp.where(diagonal, row, 0.0), axis=1, keepdims=True)


def hidden_stage(blocks, groups, up, tok, owners):
    count = len(blocks)
    width = blocks[0].shape[1]
    hidden = up[0].shape[0]
    half = width // 2
    rows = count * tok
    sizes = [g * tok for g in groups]

    def kernel(*refs):
        xs, (up0, up1) = refs[:count], refs[count : count + 2]
        act_refs = refs[count + 2 : count + 2 + len(groups)]
        slope_refs = refs[count + 2 + len(groups) : count + 2 + 2 * len(groups)]
        buffer = refs[-1]
        fill(buffer, xs, limit=tok)
        at, j = 0, 0
        for index, g in enumerate(groups):
            x = buffer[pl.ds(at, g * tok), :]
            pre = dot_rows(x[:, :half], up0[...]) + dot_rows(x[:, half:], up1[...])
            sig = 1.0 / (1.0 + jnp.exp(-pre))
            for b in range(g):
                w = weight_column(xs[j], tok, owners, lax.axis_index("expert"))
                p = pre[b * tok : (b + 1) * tok]
                s = sig[b * tok : (b + 1) * tok]
                ws = w * s
                act_refs[index][pl.ds(b * tok, tok), :] = (ws * p).astype(BF)
                slope_refs[index][pl.ds(b * tok, tok), :] = (ws * (1.0 + p * (1.0 - s))).astype(BF)
                j += 1
            at += g * tok

    outs = [shaped((size, hidden), BF) for size in sizes]
    result = vmem_call(
        kernel,
        outs + outs,
        list(blocks) + [up[0], up[1]],
        scratch=[pltpu.VMEM((rows, width), BF)],
        flops=2 * rows * width * hidden,
    )
    return result[: len(groups)], result[len(groups) :]


def project(act, down, *adds):
    total = jnp.dot(act, down, preferred_element_type=F32)
    for add in adds:
        missing = act.shape[0] - add.shape[0]
        total = total + jnp.pad(add, ((missing, 0), (0, 0))).astype(F32)
    return total


def outer_sum(lefts, rights, out_dtype, rw, start=0, limit=None):
    nl, nr = len(lefts), len(rights)
    rows = sum(a.shape[0] for a in lefts)
    lw = lefts[0].shape[1]

    def kernel(*refs):
        out_ref, left, right = refs[-3:]
        fill(left, refs[:nl])
        fill(right, refs[nl : nl + nr], start, limit)
        at = 0
        while at < lw:
            size = min(256, lw - at)
            value = lax.dot_general(
                left[:, at : at + size],
                right[...],
                (((0,), (0,)), ((), ())),
                preferred_element_type=F32,
            )
            out_ref[at : at + size, :] = value.astype(out_dtype)
            at += size

    return vmem_call(
        kernel,
        [shaped((lw, rw), out_dtype)],
        list(lefts) + list(rights),
        scratch=[pltpu.VMEM((rows, lw), BF), pltpu.VMEM((rows, rw), BF)],
        flops=2 * rows * lw * rw,
    )[0]


def back_stage(grads, slopes, down):
    count = len(slopes)
    hidden = down[0].shape[0]

    def kernel(*refs):
        g0, g1 = refs[:count], refs[count : 2 * count]
        slope = refs[2 * count : 3 * count]
        down0, down1 = refs[3 * count : 3 * count + 2]
        outs = refs[3 * count + 2 :]
        for b in range(count):
            value = dot_rows(g0[b][...], down0[...]) + dot_rows(g1[b][...], down1[...])
            outs[b][...] = (value * slope[b][...].astype(F32)).astype(BF)

    rows = sum(s.shape[0] for s in slopes)
    return vmem_call(
        kernel,
        [shaped(s.shape, BF) for s in slopes],
        list(grads[0]) + list(grads[1]) + list(slopes) + list(down),
        flops=4 * rows * down[0].shape[1] * hidden,
    )


def eye(size):
    return lax.broadcasted_iota(jnp.int32, (size, size), 0) == lax.broadcasted_iota(
        jnp.int32, (size, size), 1
    )


def to_column(row):
    return jnp.sum(jnp.where(eye(row.shape[1]), row, 0.0), axis=1, keepdims=True)


def to_row(column):
    return jnp.sum(jnp.where(eye(column.shape[0]), column, 0.0), axis=0, keepdims=True)


def clicks_of(rank_ref, click_ref, alpha_ref, beta_ref):
    rank_row = rank_ref[...]
    hot = (
        lax.broadcasted_iota(jnp.int32, (alpha_ref.shape[1], rank_row.shape[1]), 0) == rank_row
    ).astype(F32)
    alpha = jnp.sum(hot * to_column(alpha_ref[...]), axis=0, keepdims=True)
    beta = jnp.sum(hot * to_column(beta_ref[...]), axis=0, keepdims=True)
    return (click_ref[...].astype(F32) - beta) / alpha


def lists_of(list_ref, count):
    row = list_ref[...]
    return (lax.broadcasted_iota(jnp.int32, (count, row.shape[1]), 0) == row).astype(F32)


def pool_of(pool_ref, cands):
    row = pool_ref[...]
    return (lax.broadcasted_iota(jnp.int32, (cands, row.shape[1]), 0) == row).astype(F32)


def units_of(head_refs, own_ref, other_ref):
    part = head_refs[1].shape[0]
    first = lax.axis_index("expert") % 2 == 0
    low, high = other_ref[:, :part], other_ref[:, part:]
    return [own_ref[...], jnp.where(first, low, high), jnp.where(first, high, low)]


def score_stage(rolled, sums, head, out_w, lists_in):
    width = rolled.shape[1]
    tok = sums[0].shape[0]
    half = width // 2
    cands = lists_in[1].shape[1]
    units = sum(h.shape[0] for h in head)
    per_half = len(sums) // 2

    def kernel(*refs):
        rolled_ref = refs[0]
        sum_refs = refs[1 : 1 + 2 * per_half]
        rest = refs[1 + 2 * per_half :]
        head_refs, out_refs = rest[:3], rest[3:5]
        pool_ref, list_ref, click_ref, rank_ref, alpha_ref, beta_ref = rest[5:11]
        normed_ref, inv_ref, pooled_ref, act_ref, exp_ref, corr_ref, tot_ref = rest[11:]
        mixed = []
        for h in range(2):
            value = rolled_ref[:tok, h * half : (h + 1) * half].astype(F32)
            for ref in sum_refs[h * per_half : (h + 1) * per_half]:
                value = value + ref[...].astype(F32)
            mixed.append(value)
        square = sum(jnp.sum(m * m, axis=1, keepdims=True) for m in mixed)
        inv = lax.rsqrt(square * (1.0 / width) + 1e-06)
        inv_ref[...] = inv
        hot = pool_of(pool_ref, cands)
        counts = jnp.sum(hot, axis=1, keepdims=True)
        pooled = []
        for h in range(2):
            normed = mixed[h] * inv
            normed_ref[:, h * half : (h + 1) * half] = normed
            pooled.append(
                jnp.dot(
                    hot, normed, precision=lax.Precision.HIGHEST, preferred_element_type=F32
                )
                / counts
            )
        swapped = lax.axis_index("dp") != 0
        pooled_ref[:, :half] = jnp.where(swapped, pooled[1], pooled[0]).astype(BF)
        pooled_ref[:, half:] = jnp.where(swapped, pooled[0], pooled[1]).astype(BF)
        both = pooled_ref[...]
        scores = jnp.zeros((cands, 1), F32)
        at = 0
        for head_ref, out_row in zip(head_refs, units_of(head_refs, *out_refs)):
            size = head_ref.shape[0]
            act = jnp.tanh(dot_rows(both, head_ref[...]))
            act_ref[:, at : at + size] = act
            scores = scores + jnp.sum(act * out_row, axis=1, keepdims=True)
            at += size
        score_row = to_row(scores)
        exp_row = jnp.exp(score_row)
        exp_ref[...] = exp_row
        corrected = clicks_of(rank_ref, click_ref, alpha_ref, beta_ref)
        corr_ref[...] = corrected
        member = lists_of(list_ref, LISTS)
        lane = lax.broadcasted_iota(jnp.int32, (LISTS, 128), 1)
        total = jnp.zeros((LISTS, 128), F32)
        for k, row in enumerate((exp_row, corrected * score_row, corrected)):
            total = jnp.where(lane == k, jnp.sum(member * row, axis=1, keepdims=True), total)
        tot_ref[...] = total

    return vmem_call(
        kernel,
        [
            shaped((tok, width), F32),
            shaped((tok, 1), F32),
            shaped((cands, width), BF),
            shaped((cands, units), F32),
            shaped((1, cands), F32),
            shaped((1, cands), F32),
            shaped((LISTS, 128), F32),
        ],
        [rolled] + sums + head + out_w + lists_in,
        flops=4 * cands * width * units,
    )


def grad_stage(own, other, state, head, out_w, pool_ids, list_ids):
    normed, _, _, _, _, _ = state
    tok, width = normed.shape
    half = width // 2
    cands = list_ids.shape[1]

    def kernel(*refs):
        own_ref, other_ref, normed_ref, inv_ref, pooled_ref, act_ref, exp_ref, corr_ref = refs[:8]
        head_refs, out_refs = refs[8:11], refs[11:13]
        pool_ref, list_ref = refs[13:15]
        loss_ref, low_ref, high_ref, packed_ref = refs[15:]
        totals = own_ref[...] + other_ref[...]
        exp_total, cross_total, click_total = totals[:, 0:1], totals[:, 1:2], totals[:, 2:3]
        loss_ref[...] = jnp.sum(
            click_total * jnp.log(exp_total) - cross_total, axis=0, keepdims=True
        )
        member = lists_of(list_ref, LISTS)
        cand_row = (
            jnp.sum(member * (click_total / exp_total), axis=0, keepdims=True) * exp_ref[...]
            - corr_ref[...]
        )
        cand = to_column(cand_row)
        back = jnp.zeros((cands, width), F32)
        at = 0
        for head_ref, out_row in zip(head_refs, units_of(head_refs, *out_refs)):
            size = head_ref.shape[0]
            act = act_ref[:, at : at + size]
            hid = (cand * out_row * (1.0 - act * act)).astype(BF)
            back = back + jnp.dot(hid, head_ref[...], preferred_element_type=F32)
            at += size
        hot = pool_of(pool_ref, cands)
        back = back / jnp.sum(hot, axis=1, keepdims=True)
        swapped = lax.axis_index("dp") != 0
        parts = [
            jnp.where(swapped, back[:, half:], back[:, :half]),
            jnp.where(swapped, back[:, :half], back[:, half:]),
        ]
        grads = [
            lax.dot_general(
                hot,
                p,
                (((0,), (0,)), ((), ())),
                precision=lax.Precision.HIGHEST,
                preferred_element_type=F32,
            )
            for p in parts
        ]
        mean = sum(
            jnp.sum(g * normed_ref[:, h * half : (h + 1) * half], axis=1, keepdims=True)
            for h, g in enumerate(grads)
        ) * (1.0 / width)
        for h, ref in enumerate((low_ref, high_ref)):
            n = normed_ref[:, h * half : (h + 1) * half]
            ref[...] = (inv_ref[...] * (grads[h] - n * mean)).astype(BF)
        packed_ref[:, :width] = pooled_ref[...]
        top = cand.astype(BF).astype(F32)
        middle = (cand - top).astype(BF).astype(F32)
        bottom = cand - top - middle
        lane = lax.broadcasted_iota(jnp.int32, (cands, 128), 1)
        packed_ref[:, width:] = jnp.where(
            lane == 0, top, jnp.where(lane == 1, middle, jnp.where(lane == 2, bottom, 0.0))
        ).astype(BF)

    return vmem_call(
        kernel,
        [
            shaped((1, 1), F32),
            shaped((tok, half), BF),
            shaped((tok, half), BF),
            shaped((cands, width + 128), BF),
        ],
        [own, other] + list(state) + head + out_w + [pool_ids, list_ids],
        flops=4 * cands * width * sum(h.shape[0] for h in head),
    )


def head_stage(table, blocks, head, out_w):
    count = len(blocks)
    packed_width = blocks[0].shape[1]
    total = table.shape[0]
    units, width = head.shape
    each = sum(b.shape[0] for b in blocks) // total
    cands = each // 2

    def kernel(table_ref, *refs):
        block_refs = refs[:count]
        head_ref, out_ref, grad_ref, out_grad_ref, buffer = refs[count:]
        mine, plane = lax.axis_index("expert"), lax.axis_index("dp")
        j = 0
        for ref in block_refs:
            for piece in range(ref.shape[0] // each):
                at = table_ref[mine, j] * each
                for k in range(2):
                    place = pl.multiple_of(at + (plane ^ k) * cands, cands)
                    start = piece * each + k * cands
                    buffer[pl.ds(place, cands), :] = ref[start : start + cands, :]
                j += 1
        pooled = buffer[:, :width]
        act = jnp.tanh(dot_rows(pooled, head_ref[...]))
        tail = buffer[:, width:].astype(F32)
        cand = tail[:, 0:1] + tail[:, 1:2] + tail[:, 2:3]
        hid = (cand * out_ref[...] * (1.0 - act * act)).astype(BF)
        out_grad_ref[...] = jnp.sum(cand * act, axis=0, keepdims=True)
        grad_ref[...] = lax.dot_general(
            hid, pooled, (((0,), (0,)), ((), ())), preferred_element_type=F32
        )

    return vmem_call(
        kernel,
        [shaped((units, width), F32), shaped((1, units), F32)],
        [table] + blocks + [head, out_w],
        scratch=[pltpu.VMEM((total * each, packed_width), BF)],
        flops=4 * total * each * width * units,
        smem=1,
    )


def pick_half(head):
    rows = head.shape[0] // 2

    def kernel(head_ref, out_ref):
        first = lax.axis_index("expert") % 2 == 0
        out_ref[...] = jnp.where(first, head_ref[:rows, :], head_ref[rows:, :])

    return vmem_call(kernel, [shaped((rows, head.shape[1]), head.dtype)], [head])[0]


def after(value, *others):
    return lax.optimization_barrier((value,) + others)[0]


def dense_local(*args):
    return dense_step(*args)


def dense_step(
    tokens,
    route_ids,
    route_weights,
    up_weight,
    down_weight,
    head_weight,
    out_weight,
    pool_ids,
    list_ids,
    clicks,
    ranks,
    alpha_table,
    beta_table,
):
    n_exp = lax.axis_size("expert")
    ring = Ring(n_exp)
    last = ring.half
    tok, width = tokens.shape
    half = width // 2

    def across(x):
        return lax.ppermute(x, "dp", [(0, 1), (1, 0)])

    up_own, down_own = up_weight[0].T, down_weight[0].T
    up = [up_own, across(up_own)]
    rolled = pack_stage(tokens, route_ids.T, route_weights.T, n_exp)

    mine, theirs = [rolled], [ring.swap(rolled)]
    mine_swapped, theirs_swapped = [None], [None]
    for r in range(1, last + 1):
        mine.append(ring.send(mine[-1]))
        mine_swapped.append(ring.swap(mine[-1]))
        if r < last:
            theirs.append(ring.send(theirs[-1]))
            theirs_swapped.append(ring.swap(theirs[-1]))

    down = [down_own, across(down_own)]
    head_came = across(after(pick_half(head_weight), down[1]))
    head = [head_weight, head_came, ring.swap(head_came)]
    out_row = out_weight[None, :]
    out_w = [out_row, across(after(out_row, down[1]))]

    acts, slopes = [], []
    for r in range(last + 1):
        if r == 0:
            blocks, groups = [mine[0], theirs[0]], [1, 1]
        elif r < last:
            blocks = [mine[r], theirs[r], mine_swapped[r], theirs_swapped[r]]
            groups = [2, 2]
        else:
            blocks, groups = [mine[r], mine_swapped[r]], [1, 1]
        a, s = hidden_stage(blocks, groups, up, tok, n_exp)
        acts.append(a)
        slopes.append(s)

    sums = []
    for h in range(2):
        first = project(acts[last][1], down[h]).astype(BF)
        given = ring.swap(first)
        moving = project(acts[last][0], down[h], given).astype(BF)
        for r in reversed(range(1, last)):
            block = after(acts[r][0], first) if h else acts[r][0]
            given = ring.swap(project(block, down[h]).astype(BF))
            came = ring.send(moving)
            moving = project(acts[r][1], down[h], given, came).astype(BF)
        came = ring.send(moving)
        back = project(acts[0][1], down[h], came[:tok]).astype(BF)
        sums += [project(acts[0][0], down[h], came[tok:]), ring.swap(back)]

    lists_in = [pool_ids, list_ids, clicks, ranks, alpha_table[None, :], beta_table[None, :]]
    *state, totals = score_stage(rolled, sums, head, out_w, lists_in)
    list_loss, low, high, packed = grad_stage(
        totals, across(totals), state, head, out_w, pool_ids, list_ids
    )

    def gather_blocks(x):
        blocks = []
        for rounds in ring.gather(x):
            blocks += rounds
        return blocks

    grads = [None, None]
    grads[1] = gather_blocks(high)
    grads[0] = gather_blocks(low)
    flat = lambda lists: [x for part in lists for x in part]
    act_blocks, slope_blocks = flat(acts), flat(slopes)
    sent_down = across(outer_sum(act_blocks, grads[1], BF, half))
    split = 2 * (last - 1)
    early = back_stage([grads[0][:split], grads[1][:split]], slope_blocks[:split], down)
    late = back_stage([grads[0][split:], grads[1][split:]], slope_blocks[split:], down)
    pre_grads = list(early) + list(late)
    inputs = [mine[0], theirs[0]]
    for r in range(1, last):
        inputs += [mine[r], theirs[r], mine_swapped[r], theirs_swapped[r]]
    inputs += [mine[last], mine_swapped[last]]
    sent_up = across(outer_sum(pre_grads, inputs, BF, half, half, tok))
    down_local = outer_sum(act_blocks, grads[0], F32, half)
    up_local = outer_sum(pre_grads, inputs, F32, half, 0, tok)

    pair = jnp.concatenate([packed, across(packed)])
    grad_head, grad_out = head_stage(
        jnp.asarray(ring.table), gather_blocks(pair), head_weight, out_row
    )

    grad_down = (down_local + sent_down.astype(F32)).astype(BF).T[None]
    grad_up = (up_local + sent_up.astype(F32)).astype(BF).T[None]
    return (grad_up, grad_down, grad_head, grad_out[0], list_loss[0])


def solution(mesh):
    paired = mesh.shape["dp"] == 2 and mesh.shape["expert"] % 4 == 0
    return jax.shard_map(
        dense_local if paired else routed_local,
        mesh=mesh,
        in_specs=(
            P(("dp", "expert"), None),
            P(("dp", "expert"), None),
            P(("dp", "expert"), None),
            P("expert", "dp", None),
            P("expert", "dp", None),
            P("dp", None),
            P("dp"),
            P(("dp", "expert"), None),
            P(("dp", "expert"), None),
            P(("dp", "expert"), None),
            P(("dp", "expert"), None),
            P(),
            P(),
        ),
        out_specs=(
            P("expert", "dp", None),
            P("expert", "dp", None),
            P("dp", None),
            P("dp"),
            P("expert"),
        ),
        check_vma=False,
    )
```

profile of v0, /device:TPU:0, one launch (start us, length us, event | category | flops | bytes accessed | tf_op | source)
XLA Modules:
  0.0 182.0 jit_solution(2808214859369354515)
XLA Ops:
  3.6 2.6 %collective-permute-start.2 = (bf16[136,1024]{1,0:T(8,128)(2,1)S(1)}, bf16[136,1024]{1,0:T(8,128)(2,1)S(1)}, u32[]{:S(2)}, u32[]{:S(2)}) collective-permute-start(bf16[136,1024]{1,0:T(8,128)(2,1)S(1)} %shard_map.173.refs_0_.refs_10_), channel_id=1, source_target_pairs={{0,4},{1,3},{4,8},{5,1},{8,12},{9,5},{12,14},{13,9},{14,10},{15,13... | collective-permute-start | bytes 835592 | tf_op jit(solution)/shard_map/ppermute | solution.py:60
  10.7 2.1 %collective-permute-start.7 = (bf16[136,1024]{1,0:T(8,128)(2,1)S(1)}, bf16[136,1024]{1,0:T(8,128)(2,1)S(1)}, u32[]{:S(2)}, u32[]{:S(2)}) collective-permute-start(bf16[136,1024]{1,0:T(8,128)(2,1)S(1)} %collective-permute-done.2.refs_0_.refs_12_), channel_id=1, source_target_pairs={{0,4},{1,3},{4,8},{5,1},{8,12},{9,5},{12,14},{13,9},{14,10},{15,13... | collective-permute-start | bytes 835592 | tf_op jit(solution)/shard_map/ppermute | solution.py:60
  12.8 2.0 %collective-permute-done.3.refs_1_.refs_13_ = bf16[136,1024]{1,0:T(8,128)(2,1)S(1)} collective-permute-done((bf16[136,1024]{1,0:T(8,128)(2,1)S(1)}, bf16[136,1024]{1,0:T(8,128)(2,1)S(1)}, u32[]{:S(2)}, u32[]{:S(2)}) %collective-permute-start.3) | collective-permute-done | bytes 278560 | tf_op jit(solution)/shard_map/ppermute | solution.py:60
  19.1 6.4 %collective-permute-done.25.refs_19_.refs_13_ = bf16[704,512]{1,0:T(8,128)(2,1)S(1)} collective-permute-done((bf16[704,512]{1,0:T(8,128)(2,1)}, bf16[704,512]{1,0:T(8,128)(2,1)S(1)}, u32[]{:S(2)}, u32[]{:S(2)}) %collective-permute-start.25) | collective-permute-done | bytes 720928 | tf_op jit(solution)/shard_map/ppermute | solution.py:722
  27.1 12.9 %collective-permute-done.1.refs_3_.refs_5_ = bf16[704,512]{1,0:T(8,128)(2,1)S(1)} collective-permute-done((bf16[704,512]{1,0:T(8,128)(2,1)}, bf16[704,512]{1,0:T(8,128)(2,1)S(1)}, u32[]{:S(2)}, u32[]{:S(2)}) %collective-permute-start.1) | collective-permute-done | bytes 720928 | tf_op jit(solution)/shard_map/ppermute | solution.py:722
  45.9 2.2 %collective-permute-done.13.refs_1_.refs_21_ = bf16[136,1024]{1,0:T(8,128)(2,1)S(1)} collective-permute-done((bf16[136,1024]{1,0:T(8,128)(2,1)S(1)}, bf16[136,1024]{1,0:T(8,128)(2,1)S(1)}, u32[]{:S(2)}, u32[]{:S(2)}) %collective-permute-start.13) | collective-permute-done | bytes 278560 | tf_op jit(solution)/shard_map/ppermute | solution.py:60
  58.8 3.1 %collective-permute-done.20 = bf16[128,512]{1,0:T(8,128)(2,1)S(1)} collective-permute-done((bf16[128,512]{1,0:T(8,128)(2,1)S(1)}, bf16[128,512]{1,0:T(8,128)(2,1)S(1)}, u32[]{:S(2)}, u32[]{:S(2)}) %collective-permute-start.20) | collective-permute-done | bytes 131104 | tf_op jit(solution)/shard_map/ppermute | solution.py:60
  63.7 3.1 %collective-permute-done.30 = bf16[128,512]{1,0:T(8,128)(2,1)S(1)} collective-permute-done((bf16[128,512]{1,0:T(8,128)(2,1)S(1)}, bf16[128,512]{1,0:T(8,128)(2,1)S(1)}, u32[]{:S(2)}, u32[]{:S(2)}) %collective-permute-start.30) | collective-permute-done | bytes 131104 | tf_op jit(solution)/shard_map/ppermute | solution.py:60
  68.7 4.5 %collective-permute-done.21 = bf16[256,512]{1,0:T(8,128)(2,1)S(1)} collective-permute-done((bf16[256,512]{1,0:T(8,128)(2,1)S(1)}, bf16[256,512]{1,0:T(8,128)(2,1)S(1)}, u32[]{:S(2)}, u32[]{:S(2)}) %collective-permute-start.21) | collective-permute-done | bytes 262176 | tf_op jit(solution)/shard_map/ppermute | solution.py:60
  75.1 4.5 %collective-permute-done.31 = bf16[256,512]{1,0:T(8,128)(2,1)S(1)} collective-permute-done((bf16[256,512]{1,0:T(8,128)(2,1)S(1)}, bf16[256,512]{1,0:T(8,128)(2,1)S(1)}, u32[]{:S(2)}, u32[]{:S(2)}) %collective-permute-start.31) | collective-permute-done | bytes 262176 | tf_op jit(solution)/shard_map/ppermute | solution.py:60
  83.0 3.0 %collective-permute-done.22 = bf16[256,512]{1,0:T(8,128)(2,1)S(1)} collective-permute-done((bf16[256,512]{1,0:T(8,128)(2,1)S(1)}, bf16[256,512]{1,0:T(8,128)(2,1)S(1)}, u32[]{:S(2)}, u32[]{:S(2)}) %collective-permute-start.22) | collective-permute-done | bytes 262176 | tf_op jit(solution)/shard_map/ppermute | solution.py:60
  93.2 2.6 %collective-permute-done.33 = bf16[256,512]{1,0:T(8,128)(2,1)S(1)} collective-permute-done((bf16[256,512]{1,0:T(8,128)(2,1)S(1)}, bf16[256,512]{1,0:T(8,128)(2,1)S(1)}, u32[]{:S(2)}, u32[]{:S(2)}) %collective-permute-start.33) | collective-permute-done | bytes 262176 | tf_op jit(solution)/shard_map/ppermute | solution.py:60
  100.6 1.9 %collective-permute-done.38.refs_1_ = f32[8,128]{1,0:T(8,128)S(1)} collective-permute-done((f32[8,128]{1,0:T(8,128)S(1)}, f32[8,128]{1,0:T(8,128)S(1)}, u32[]{:S(2)}, u32[]{:S(2)}) %collective-permute-start.38) | collective-permute-done | bytes 4128 | tf_op jit(solution)/shard_map/ppermute | solution.py:722
  110.1 1.9 %collective-permute-done.40.refs_2_.refs_12_ = bf16[256,512]{1,0:T(8,128)(2,1)S(1)} collective-permute-done((bf16[256,512]{1,0:T(8,128)(2,1)S(1)}, bf16[256,512]{1,0:T(8,128)(2,1)S(1)}, u32[]{:S(2)}, u32[]{:S(2)}) %collective-permute-start.40) | collective-permute-done | bytes 262176 | tf_op jit(solution)/shard_map/ppermute | solution.py:60
  116.2 2.1 %collective-permute-done.42.refs_4_.refs_14_ = bf16[256,512]{1,0:T(8,128)(2,1)S(1)} collective-permute-done((bf16[256,512]{1,0:T(8,128)(2,1)S(1)}, bf16[256,512]{1,0:T(8,128)(2,1)S(1)}, u32[]{:S(2)}, u32[]{:S(2)}) %collective-permute-start.42) | collective-permute-done | bytes 262176 | tf_op jit(solution)/shard_map/ppermute | solution.py:60
  124.7 4.4 %collective-permute-done.61.refs_2_ = bf16[64,1152]{1,0:T(8,128)(2,1)S(1)} collective-permute-done((bf16[64,1152]{1,0:T(8,128)(2,1)S(1)}, bf16[64,1152]{1,0:T(8,128)(2,1)S(1)}, u32[]{:S(2)}, u32[]{:S(2)}) %collective-permute-start.61) | collective-permute-done | bytes 147488 | tf_op jit(solution)/shard_map/ppermute | solution.py:60
  131.0 3.3 %collective-permute-done.63.refs_4_ = bf16[64,1152]{1,0:T(8,128)(2,1)S(1)} collective-permute-done((bf16[64,1152]{1,0:T(8,128)(2,1)S(1)}, bf16[64,1152]{1,0:T(8,128)(2,1)S(1)}, u32[]{:S(2)}, u32[]{:S(2)}) %collective-permute-start.63) | collective-permute-done | bytes 147488 | tf_op jit(solution)/shard_map/ppermute | solution.py:60
  140.6 2.6 %shard_map.182 = (bf16[128,704]{1,0:T(8,128)(2,1)S(1)}, bf16[128,704]{1,0:T(8,128)(2,1)S(1)}, bf16[256,704]{1,0:T(8,128)(2,1)S(1)}, bf16[256,704]{1,0:T(8,128)(2...) custom-call(bf16[128,512]{1,0:T(8,128)(2,1)S(1)} %get-tuple-element.75.refs_0_.refs_10_, ...), custom_call_target="tpu_custom_call" | custom-call | flops 1845493760 | bytes 7667712 | tf_op jit(solution)/shard_map/pallas_call | solution.py:274
  143.3 1.8 shard_map.183
  146.9 1.7 collective-permute-start.57
  150.8 2.5 %collective-permute-done.67.refs_8_ = bf16[32,1152]{1,0:T(8,128)(2,1)S(1)} collective-permute-done((bf16[32,1152]{1,0:T(8,128)(2,1)S(1)}, bf16[32,1152]{1,0:T(8,128)(2,1)S(1)}, u32[]{:S(2)}, u32[]{:S(2)}) %collective-permute-start.67) | collective-permute-done | bytes 73760 | tf_op jit(solution)/shard_map/ppermute | solution.py:60
  155.4 3.5 %shard_map.188 = (f32[512,1024]{1,0:T(8,128)}, f32[1,512]{1,0:T(1,128)}) custom-call(s32[16,16]{1,0:T(8,128)S(1)} %copy-done.14, bf16[32,1152]{1,0:T(8,128)(2,1)S(1)} %constant_dynamic-update-slice_fusion.refs_0_, bf16[32,1152]{1,0:T(8,128)(2,1)S(1)} %collective-permute-done.60.refs_1_, bf16[64,1152]{1,0:T(8,128)(2,1)S(1)} %collective-permute-done.61.refs_2_, ...), custom_call_target="tpu_custom_call" | custom-call | flops 1073741824 | bytes 4330496 | tf_op jit(solution)/shard_map/pallas_call | solution.py:274
  162.4 3.5 %collective-permute-done.57 = bf16[704,512]{1,0:T(8,128)(2,1)S(1)} collective-permute-done((bf16[704,512]{1,0:T(8,128)(2,1)S(1)}, bf16[704,512]{1,0:T(8,128)(2,1)S(1)}, u32[]{:S(2)}, u32[]{:S(2)}) %collective-permute-start.57) | collective-permute-done | bytes 720928 | tf_op jit(solution)/shard_map/ppermute | solution.py:722
  167.0 13.9 %collective-permute-done.58 = bf16[704,512]{1,0:T(8,128)(2,1)S(1)} collective-permute-done((bf16[704,512]{1,0:T(8,128)(2,1)S(1)}, bf16[704,512]{1,0:T(8,128)(2,1)S(1)}, u32[]{:S(2)}, u32[]{:S(2)}) %collective-permute-start.58) | collective-permute-done | bytes 720928 | tf_op jit(solution)/shard_map/ppermute | solution.py:722
  (190 shorter events, 88.3 us)
Async XLA Ops:
  3.6 7.1 %collective-permute-start.2 = (bf16[136,1024]{1,0:T(8,128)(2,1)S(1)}, bf16[136,1024]{1,0:T(8,128)(2,1)S(1)}, u32[]{:S(2)}, u32[]{:S(2)}) collective-permute-start(bf16[136,1024]{1,0:T(8,128)(2,1)S(1)} %shard_map.173.refs_0_.refs_10_), channel_id=1, source_target_pairs={{0,4},{1,3},{4,8},{5,1},{8,12},{9,5},{12,14},{13,9},{14,10},{15,13... | collective-permute-start | bytes 835592 | tf_op jit(solution)/shard_map/ppermute | solution.py:60
  6.2 19.2 %collective-permute-start.25 = (bf16[704,512]{1,0:T(8,128)(2,1)}, bf16[704,512]{1,0:T(8,128)(2,1)S(1)}, u32[]{:S(2)}, u32[]{:S(2)}) collective-permute-start(bf16[704,512]{1,0:T(8,128)(2,1)} %bitcast.71), channel_id=1, source_target_pairs={{0,16},{16,0},{1,17},{17,1},{2,18},{18,2},{3,19},{19,3},{4,20},{20... | collective-permute-start | bytes 2162696 | tf_op jit(solution)/shard_map/ppermute | solution.py:722
  7.7 32.3 %collective-permute-start.1 = (bf16[704,512]{1,0:T(8,128)(2,1)}, bf16[704,512]{1,0:T(8,128)(2,1)S(1)}, u32[]{:S(2)}, u32[]{:S(2)}) collective-permute-start(bf16[704,512]{1,0:T(8,128)(2,1)} %bitcast.74), channel_id=1, source_target_pairs={{0,16},{16,0},{1,17},{17,1},{2,18},{18,2},{3,19},{19,3},{4,20},{20... | collective-permute-start | bytes 2162696 | tf_op jit(solution)/shard_map/ppermute | solution.py:722
  12.7 12.7 %collective-permute-start.4 = (bf16[136,1024]{1,0:T(8,128)(2,1)S(1)}, bf16[136,1024]{1,0:T(8,128)(2,1)S(1)}, u32[]{:S(2)}, u32[]{:S(2)}) collective-permute-start(bf16[136,1024]{1,0:T(8,128)(2,1)S(1)} %collective-permute-done.2.refs_0_.refs_12_), channel_id=1, source_target_pairs={{0,1},{1,0},{2,3},{3,2},{4,5},{5,4},{6,7},{7,6},{8,9},{9,8},{10,11... | collective-permute-start | bytes 835592 | tf_op jit(solution)/shard_map/ppermute | solution.py:63
  14.8 26.7 %collective-permute-start.8 = (bf16[136,1024]{1,0:T(8,128)(2,1)S(1)}, bf16[136,1024]{1,0:T(8,128)(2,1)S(1)}, u32[]{:S(2)}, u32[]{:S(2)}) collective-permute-start(bf16[136,1024]{1,0:T(8,128)(2,1)S(1)} %collective-permute-done.3.refs_1_.refs_13_), channel_id=1, source_target_pairs={{0,4},{1,3},{4,8},{5,1},{8,12},{9,5},{12,14},{13,9},{14,10},{15,13... | collective-permute-start | bytes 835592 | tf_op jit(solution)/shard_map/ppermute | solution.py:60
  17.8 23.7 %collective-permute-start.5 = (bf16[136,1024]{1,0:T(8,128)(2,1)S(1)}, bf16[136,1024]{1,0:T(8,128)(2,1)S(1)}, u32[]{:S(2)}, u32[]{:S(2)}) collective-permute-start(bf16[136,1024]{1,0:T(8,128)(2,1)S(1)} %collective-permute-done.3.refs_1_.refs_13_), channel_id=1, source_target_pairs={{0,1},{1,0},{2,3},{3,2},{4,5},{5,4},{6,7},{7,6},{8,9},{9,8},{10,11... | collective-permute-start | bytes 835592 | tf_op jit(solution)/shard_map/ppermute | solution.py:63
  25.4 18.2 %collective-permute-start.9 = (bf16[136,1024]{1,0:T(8,128)(2,1)S(1)}, bf16[136,1024]{1,0:T(8,128)(2,1)S(1)}, u32[]{:S(2)}, u32[]{:S(2)}) collective-permute-start(bf16[136,1024]{1,0:T(8,128)(2,1)S(1)} %collective-permute-done.7.refs_0_.refs_16_), channel_id=1, source_target_pairs={{0,1},{1,0},{2,3},{3,2},{4,5},{5,4},{6,7},{7,6},{8,9},{9,8},{10,11... | collective-permute-start | bytes 835592 | tf_op jit(solution)/shard_map/ppermute | solution.py:63
  25.4 18.7 %collective-permute-start.12 = (bf16[136,1024]{1,0:T(8,128)(2,1)S(1)}, bf16[136,1024]{1,0:T(8,128)(2,1)S(1)}, u32[]{:S(2)}, u32[]{:S(2)}) collective-permute-start(bf16[136,1024]{1,0:T(8,128)(2,1)S(1)} %collective-permute-done.7.refs_0_.refs_16_), channel_id=1, source_target_pairs={{0,4},{1,3},{4,8},{5,1},{8,12},{9,5},{12,14},{13,9},{14,10},{15,13... | collective-permute-start | bytes 835592 | tf_op jit(solution)/shard_map/ppermute | solution.py:60
  40.0 51.9 %collective-permute-start.35 = (bf16[256,1024]{1,0:T(8,128)(2,1)S(1)}, bf16[256,1024]{1,0:T(8,128)(2,1)S(1)}, u32[]{:S(2)}, u32[]{:S(2)}) collective-permute-start(bf16[256,1024]{1,0:T(8,128)(2,1)S(1)} %shard_map.179), channel_id=1, source_target_pairs={{0,16},{16,0},{1,17},{17,1},{2,18},{18,2},{3,19},{19,3},{4,20},{20... | collective-permute-start | bytes 1572872 | tf_op jit(solution)/shard_map/ppermute | solution.py:722
  43.7 53.1 %collective-permute-start.37 = (f32[1,512]{1,0:T(1,128)S(1)}, f32[1,512]{1,0:T(1,128)S(1)}, u32[]{:S(2)}, u32[]{:S(2)}) collective-permute-start(f32[1,512]{1,0:T(1,128)S(1)} %bitcast.80), channel_id=1, source_target_pairs={{0,16},{16,0},{1,17},{17,1},{2,18},{18,2},{3,19},{19,3},{4,20},{20... | collective-permute-start | bytes 6152 | tf_op jit(solution)/shard_map/ppermute | solution.py:722
  49.7 31.7 %collective-permute-start.6 = (bf16[256,512]{1,0:T(8,128)(2,1)S(1)}, bf16[256,512]{1,0:T(8,128)(2,1)S(1)}, u32[]{:S(2)}, u32[]{:S(2)}) collective-permute-start(bf16[256,512]{1,0:T(8,128)(2,1)S(1)} %convolution_convert_fusion.5), channel_id=1, source_target_pairs={{0,1},{1,0},{2,3},{3,2},{4,5},{5,4},{6,7},{7,6},{8,9},{9,8},{10,11... | collective-permute-start | bytes 786440 | tf_op jit(solution)/shard_map/ppermute | solution.py:63
  75.0 12.8 %collective-permute-start.26 = (bf16[256,512]{1,0:T(8,128)(2,1)S(1)}, bf16[256,512]{1,0:T(8,128)(2,1)S(1)}, u32[]{:S(2)}, u32[]{:S(2)}) collective-permute-start(bf16[256,512]{1,0:T(8,128)(2,1)S(1)} %convolution_convert_fusion.2), channel_id=1, source_target_pairs={{0,1},{1,0},{2,3},{3,2},{4,5},{5,4},{6,7},{7,6},{8,9},{9,8},{10,11... | collective-permute-start | bytes 786440 | tf_op jit(solution)/shard_map/ppermute | solution.py:63
  81.4 7.4 %collective-permute-start.32 = (bf16[256,512]{1,0:T(8,128)(2,1)S(1)}, bf16[256,512]{1,0:T(8,128)(2,1)S(1)}, u32[]{:S(2)}, u32[]{:S(2)}) collective-permute-start(bf16[256,512]{1,0:T(8,128)(2,1)S(1)} %fusion.10), channel_id=1, source_target_pairs={{0,4},{1,3},{4,8},{5,1},{8,12},{9,5},{12,14},{13,9},{14,10},{15,13... | collective-permute-start | bytes 786440 | tf_op jit(solution)/shard_map/ppermute | solution.py:60
  107.0 7.8 %collective-permute-start.45 = (bf16[256,512]{1,0:T(8,128)(2,1)S(1)}, bf16[256,512]{1,0:T(8,128)(2,1)S(1)}, u32[]{:S(2)}, u32[]{:S(2)}) collective-permute-start(bf16[256,512]{1,0:T(8,128)(2,1)S(1)} %pad_maximum_fusion.1), channel_id=1, source_target_pairs={{0,4},{1,3},{4,8},{5,1},{8,12},{9,5},{12,14},{13,9},{14,10},{15,13... | collective-permute-start | bytes 786440 | tf_op jit(solution)/shard_map/ppermute | solution.py:60
  108.6 7.5 %collective-permute-start.59 = (bf16[16,1152]{1,0:T(8,128)(2,1)S(1)}, bf16[16,1152]{1,0:T(8,128)(2,1)S(1)}, u32[]{:S(2)}, u32[]{:S(2)}) collective-permute-start(bf16[16,1152]{1,0:T(8,128)(2,1)S(1)} %get-tuple-element.97), channel_id=1, source_target_pairs={{0,16},{16,0},{1,17},{17,1},{2,18},{18,2},{3,19},{19,3},{4,20},{20... | collective-permute-start | bytes 110600 | tf_op jit(solution)/shard_map/ppermute | solution.py:722
  118.3 10.8 %collective-permute-start.49 = (bf16[256,512]{1,0:T(8,128)(2,1)S(1)}, bf16[256,512]{1,0:T(8,128)(2,1)S(1)}, u32[]{:S(2)}, u32[]{:S(2)}) collective-permute-start(bf16[256,512]{1,0:T(8,128)(2,1)S(1)} %collective-permute-done.42.refs_4_.refs_14_), channel_id=1, source_target_pairs={{0,4},{1,3},{4,8},{5,1},{8,12},{9,5},{12,14},{13,9},{14,10},{15,13... | collective-permute-start | bytes 786440 | tf_op jit(solution)/shard_map/ppermute | solution.py:60
  121.2 9.3 %collective-permute-start.53 = (bf16[256,512]{1,0:T(8,128)(2,1)S(1)}, bf16[256,512]{1,0:T(8,128)(2,1)S(1)}, u32[]{:S(2)}, u32[]{:S(2)}) collective-permute-start(bf16[256,512]{1,0:T(8,128)(2,1)S(1)} %collective-permute-done.47.refs_10_.refs_14_), channel_id=1, source_target_pairs={{0,4},{1,3},{4,8},{5,1},{8,12},{9,5},{12,14},{13,9},{14,10},{15,13... | collective-permute-start | bytes 786440 | tf_op jit(solution)/shard_map/ppermute | solution.py:60
  124.2 11.5 %collective-permute-start.41 = (bf16[256,512]{1,0:T(8,128)(2,1)S(1)}, bf16[256,512]{1,0:T(8,128)(2,1)S(1)}, u32[]{:S(2)}, u32[]{:S(2)}) collective-permute-start(bf16[256,512]{1,0:T(8,128)(2,1)S(1)} %collective-permute-done.40.refs_2_.refs_12_), channel_id=1, source_target_pairs={{0,1},{1,0},{2,3},{3,2},{4,5},{5,4},{6,7},{7,6},{8,9},{9,8},{10,11... | collective-permute-start | bytes 786440 | tf_op jit(solution)/shard_map/ppermute | solution.py:63
  124.2 13.0 %collective-permute-start.46 = (bf16[256,512]{1,0:T(8,128)(2,1)S(1)}, bf16[256,512]{1,0:T(8,128)(2,1)S(1)}, u32[]{:S(2)}, u32[]{:S(2)}) collective-permute-start(bf16[256,512]{1,0:T(8,128)(2,1)S(1)} %collective-permute-done.45.refs_8_.refs_12_), channel_id=1, source_target_pairs={{0,1},{1,0},{2,3},{3,2},{4,5},{5,4},{6,7},{7,6},{8,9},{9,8},{10,11... | collective-permute-start | bytes 786440 | tf_op jit(solution)/shard_map/ppermute | solution.py:63
  129.1 8.1 %collective-permute-start.43 = (bf16[256,512]{1,0:T(8,128)(2,1)S(1)}, bf16[256,512]{1,0:T(8,128)(2,1)S(1)}, u32[]{:S(2)}, u32[]{:S(2)}) collective-permute-start(bf16[256,512]{1,0:T(8,128)(2,1)S(1)} %collective-permute-done.42.refs_4_.refs_14_), channel_id=1, source_target_pairs={{0,1},{1,0},{2,3},{3,2},{4,5},{5,4},{6,7},{7,6},{8,9},{9,8},{10,11... | collective-permute-start | bytes 786440 | tf_op jit(solution)/shard_map/ppermute | solution.py:63
  130.5 7.2 %collective-permute-start.48 = (bf16[256,512]{1,0:T(8,128)(2,1)S(1)}, bf16[256,512]{1,0:T(8,128)(2,1)S(1)}, u32[]{:S(2)}, u32[]{:S(2)}) collective-permute-start(bf16[256,512]{1,0:T(8,128)(2,1)S(1)} %collective-permute-done.47.refs_10_.refs_14_), channel_id=1, source_target_pairs={{0,1},{1,0},{2,3},{3,2},{4,5},{5,4},{6,7},{7,6},{8,9},{9,8},{10,11... | collective-permute-start | bytes 786440 | tf_op jit(solution)/shard_map/ppermute | solution.py:63
  137.7 10.9 %collective-permute-start.65 = (bf16[64,1152]{1,0:T(8,128)(2,1)S(1)}, bf16[64,1152]{1,0:T(8,128)(2,1)S(1)}, u32[]{:S(2)}, u32[]{:S(2)}) collective-permute-start(bf16[64,1152]{1,0:T(8,128)(2,1)S(1)} %collective-permute-done.63.refs_4_), channel_id=1, source_target_pairs={{0,4},{1,3},{4,8},{5,1},{8,12},{9,5},{12,14},{13,9},{14,10},{15,13... | collective-permute-start | bytes 442376 | tf_op jit(solution)/shard_map/ppermute | solution.py:60
  146.9 19.1 %collective-permute-start.57 = (bf16[704,512]{1,0:T(8,128)(2,1)S(1)}, bf16[704,512]{1,0:T(8,128)(2,1)S(1)}, u32[]{:S(2)}, u32[]{:S(2)}) collective-permute-start(bf16[704,512]{1,0:T(8,128)(2,1)S(1)} %shard_map.185), channel_id=1, source_target_pairs={{0,16},{16,0},{1,17},{17,1},{2,18},{18,2},{3,19},{19,3},{4,20},{20... | collective-permute-start | bytes 2162696 | tf_op jit(solution)/shard_map/ppermute | solution.py:722
  155.0 25.9 %collective-permute-start.58 = (bf16[704,512]{1,0:T(8,128)(2,1)S(1)}, bf16[704,512]{1,0:T(8,128)(2,1)S(1)}, u32[]{:S(2)}, u32[]{:S(2)}) collective-permute-start(bf16[704,512]{1,0:T(8,128)(2,1)S(1)} %shard_map.187), channel_id=1, source_target_pairs={{0,16},{16,0},{1,17},{17,1},{2,18},{18,2},{3,19},{19,3},{4,20},{20... | collective-permute-start | bytes 2162696 | tf_op jit(solution)/shard_map/ppermute | solution.py:722
  (60 other events, 301.5 us)
where the time goes:
time: 182 us
  waiting for transfers between devices  89 us (49%)
  starting transfers between devices  55.6 us (31%)
  Pallas kernels  23.6 us (13%)
  matrix products  6.59 us (4%)
  local copies, waits for them, and re-layouts  3.63 us (2%)
  other arithmetic  2.23 us (1%)
    ppermute x27, waiting for transfers between devices, send(): return lax.ppermute(x, 'expert', self.forward)  48.5 us
    ppermute x27, starting transfers between devices, send(): return lax.ppermute(x, 'expert', self.forward)  40.5 us
    ppermute x8, waiting for transfers between devices, across(): return lax.ppermute(x, 'dp', [(0, 1), (1, 0)])  38.7 us
    pallas_call x16, Pallas kernels, vmem_call(): pl.pallas_call(kernel, out_shape=outs, in_specs=specs, out_specs=[pl.Bloc...  23.6 us
    ppermute x8, starting transfers between devices, across(): return lax.ppermute(x, 'dp', [(0, 1), (1, 0)])  9.27 us
    dot_general x20, matrix products, project(): total = jnp.dot(act, down, preferred_element_type=F32)  6.59 us
    ppermute x34, starting transfers between devices, swap(): return lax.ppermute(x, 'expert', self.swap_pairs)  5.83 us
  transfers between devices with their start and end apart: 69, of which 29 were waited for; matrix products, arithmetic and copies ran while one was open for 4% of the time, Pallas kernels for 11%

commit v1 on v0

--- a/solution.py
+++ b/solution.py
@@ -254,6 +254,7 @@
 
 
 SPARE_VMEM = 6 * 1024 * 1024
+WIDE_GRANT = 63 * 1024 * 1024
 
 
 def padded_bytes(x):
@@ -262,11 +263,15 @@
     return lead * rows * (-(-x.shape[-1] // 128) * 128) * x.dtype.itemsize
 
 
-def vmem_call(kernel, outs, args, scratch=(), flops=0, smem=0):
+def vmem_call(kernel, outs, args, scratch=(), flops=0, smem=0, grant=None):
     held = sum(padded_bytes(a) for a in list(args)[smem:] + list(outs))
-    held += sum(int(np.prod(b.shape)) * jnp.dtype(b.dtype).itemsize for b in scratch)
+    held += sum(
+        int(np.prod(b.shape)) * jnp.dtype(b.dtype).itemsize
+        for b in scratch
+        if b.memory_space == pltpu.VMEM
+    )
     specs = [pl.BlockSpec(memory_space=pltpu.SMEM)] * smem + [
-        pl.BlockSpec(memory_space=pltpu.VMEM)
+        pl.BlockSpec(memory_space=pltpu.HBM if grant else pltpu.VMEM)
     ] * (len(args) - smem)
     moved = sum(a.size * a.dtype.itemsize for a in args) + sum(
         o.size * o.dtype.itemsize for o in outs
@@ -278,7 +283,7 @@
         out_specs=[pl.BlockSpec(memory_space=pltpu.VMEM)] * len(outs),
         scratch_shapes=list(scratch),
         cost_estimate=pl.CostEstimate(flops=flops, bytes_accessed=moved, transcendentals=0),
-        compiler_params=pltpu.CompilerParams(vmem_limit_bytes=held + SPARE_VMEM),
+        compiler_params=pltpu.CompilerParams(vmem_limit_bytes=grant or held + SPARE_VMEM),
     )(*args)
 
 
@@ -306,7 +311,17 @@
     extra = 2 * -(-owners // per_row)
     rows = tok + -(-extra // 8) * 8
 
-    def kernel(tok_ref, id_ref, weight_ref, out_ref):
+    def kernel(tok_hbm, id_hbm, weight_hbm, out_ref, tok_ref, id_ref, weight_ref, sems):
+        pulls = [
+            pltpu.make_async_copy(source, target, sems.at[k])
+            for k, (source, target) in enumerate(
+                ((id_hbm, id_ref), (weight_hbm, weight_ref), (tok_hbm, tok_ref))
+            )
+        ]
+        for pull in pulls:
+            pull.start()
+        for pull in pulls:
+            pull.wait()
         swapped = lax.axis_index("dp") != 0
         out_ref[:tok, :half] = jnp.where(swapped, tok_ref[:, half:], tok_ref[:, :half])
         out_ref[:tok, half:] = jnp.where(swapped, tok_ref[:, :half], tok_ref[:, half:])
@@ -327,7 +342,18 @@
         filled.append(jnp.zeros((rows - tok - extra, width), F32))
         out_ref[tok:, :] = jnp.concatenate(filled, axis=0).astype(BF)
 
-    return vmem_call(kernel, [shaped((rows, width), BF)], [tokens, ids, weights])[0]
+    return vmem_call(
+        kernel,
+        [shaped((rows, width), BF)],
+        [tokens, ids, weights],
+        scratch=[
+            pltpu.VMEM(tokens.shape, tokens.dtype),
+            pltpu.VMEM(ids.shape, ids.dtype),
+            pltpu.VMEM(weights.shape, weights.dtype),
+            pltpu.SemaphoreType.DMA((3,)),
+        ],
+        grant=WIDE_GRANT,
+    )[0]
 
 
 def weight_column(ref, tok, owners, mine):
@@ -393,7 +419,7 @@
     return total
 
 
-def outer_sum(lefts, rights, out_dtype, rw, start=0, limit=None):
+def outer_sum(lefts, rights, out_dtype, rw, start=0, limit=None, base=None):
     nl, nr = len(lefts), len(rights)
     rows = sum(a.shape[0] for a in lefts)
     lw = lefts[0].shape[1]
@@ -411,13 +437,15 @@
                 (((0,), (0,)), ((), ())),
                 preferred_element_type=F32,
             )
+            if base is not None:
+                value = value + refs[nl + nr][at : at + size, :]
             out_ref[at : at + size, :] = value.astype(out_dtype)
             at += size
 
     return vmem_call(
         kernel,
         [shaped((lw, rw), out_dtype)],
-        list(lefts) + list(rights),
+        list(lefts) + list(rights) + ([] if base is None else [base]),
         scratch=[pltpu.VMEM((rows, lw), BF), pltpu.VMEM((rows, rw), BF)],
         flops=2 * rows * lw * rw,
     )[0]
@@ -562,34 +590,18 @@
     )
 
 
-def grad_stage(own, other, state, head, out_w, pool_ids, list_ids):
-    normed, _, _, _, _, _ = state
+def slope_stage(normed, inv, head_act, head, out_w, pool_ids, cands):
     tok, width = normed.shape
     half = width // 2
-    cands = list_ids.shape[1]
-
-    def kernel(*refs):
-        own_ref, other_ref, normed_ref, inv_ref, pooled_ref, act_ref, exp_ref, corr_ref = refs[:8]
-        head_refs, out_refs = refs[8:11], refs[11:13]
-        pool_ref, list_ref = refs[13:15]
-        loss_ref, low_ref, high_ref, packed_ref = refs[15:]
-        totals = own_ref[...] + other_ref[...]
-        exp_total, cross_total, click_total = totals[:, 0:1], totals[:, 1:2], totals[:, 2:3]
-        loss_ref[...] = jnp.sum(
-            click_total * jnp.log(exp_total) - cross_total, axis=0, keepdims=True
-        )
-        member = lists_of(list_ref, LISTS)
-        cand_row = (
-            jnp.sum(member * (click_total / exp_total), axis=0, keepdims=True) * exp_ref[...]
-            - corr_ref[...]
-        )
-        cand = to_column(cand_row)
+
+    def kernel(normed_ref, inv_ref, act_ref, *refs):
+        head_refs, out_refs, pool_ref, slope_ref = refs[:3], refs[3:5], refs[5], refs[6]
         back = jnp.zeros((cands, width), F32)
         at = 0
         for head_ref, out_row in zip(head_refs, units_of(head_refs, *out_refs)):
             size = head_ref.shape[0]
             act = act_ref[:, at : at + size]
-            hid = (cand * out_row * (1.0 - act * act)).astype(BF)
+            hid = (out_row * (1.0 - act * act)).astype(BF)
             back = back + jnp.dot(hid, head_ref[...], preferred_element_type=F32)
             at += size
         hot = pool_of(pool_ref, cands)
@@ -613,9 +625,41 @@
             jnp.sum(g * normed_ref[:, h * half : (h + 1) * half], axis=1, keepdims=True)
             for h, g in enumerate(grads)
         ) * (1.0 / width)
-        for h, ref in enumerate((low_ref, high_ref)):
-            n = normed_ref[:, h * half : (h + 1) * half]
-            ref[...] = (inv_ref[...] * (grads[h] - n * mean)).astype(BF)
+        for h in range(2):
+            at = slice(h * half, (h + 1) * half)
+            slope_ref[:, at] = inv_ref[...] * (grads[h] - normed_ref[:, at] * mean)
+
+    return vmem_call(
+        kernel,
+        [shaped((tok, width), F32)],
+        [normed, inv, head_act] + head + out_w + [pool_ids],
+        flops=2 * cands * width * sum(h.shape[0] for h in head),
+    )[0]
+
+
+def grad_stage(own, other, slope, pooled, exp_row, corrected, pool_ids, list_ids):
+    tok, width = slope.shape
+    half = width // 2
+    cands = list_ids.shape[1]
+
+    def kernel(*refs):
+        own_ref, other_ref, slope_ref, pooled_ref, exp_ref, corr_ref, pool_ref, list_ref = refs[:8]
+        loss_ref, low_ref, high_ref, packed_ref = refs[8:]
+        totals = own_ref[...] + other_ref[...]
+        exp_total, cross_total, click_total = totals[:, 0:1], totals[:, 1:2], totals[:, 2:3]
+        loss_ref[...] = jnp.sum(
+            click_total * jnp.log(exp_total) - cross_total, axis=0, keepdims=True
+        )
+        member = lists_of(list_ref, LISTS)
+        cand_row = (
+            jnp.sum(member * (click_total / exp_total), axis=0, keepdims=True) * exp_ref[...]
+            - corr_ref[...]
+        )
+        cand = to_column(cand_row)
+        hot = pool_of(pool_ref, cands)
+        of_token = to_column(jnp.sum(hot * cand, axis=0, keepdims=True))
+        low_ref[...] = (of_token * slope_ref[:, :half]).astype(BF)
+        high_ref[...] = (of_token * slope_ref[:, half:]).astype(BF)
         packed_ref[:, :width] = pooled_ref[...]
         top = cand.astype(BF).astype(F32)
         middle = (cand - top).astype(BF).astype(F32)
@@ -633,8 +677,7 @@
             shaped((tok, half), BF),
             shaped((cands, width + 128), BF),
         ],
-        [own, other] + list(state) + head + out_w + [pool_ids, list_ids],
-        flops=4 * cands * width * sum(h.shape[0] for h in head),
+        [own, other, slope, pooled, exp_row, corrected, pool_ids, list_ids],
     )
 
 
@@ -717,6 +760,7 @@
     last = ring.half
     tok, width = tokens.shape
     half = width // 2
+    cands = list_ids.shape[1]
 
     def across(x):
         return lax.ppermute(x, "dp", [(0, 1), (1, 0)])
@@ -735,10 +779,10 @@
             theirs_swapped.append(ring.swap(theirs[-1]))
 
     down = [down_own, across(down_own)]
-    head_came = across(after(pick_half(head_weight), down[1]))
+    head_came = across(pick_half(head_weight))
     head = [head_weight, head_came, ring.swap(head_came)]
     out_row = out_weight[None, :]
-    out_w = [out_row, across(after(out_row, down[1]))]
+    out_w = [out_row, across(out_row)]
 
     acts, slopes = [], []
     for r in range(last + 1):
@@ -759,7 +803,7 @@
         given = ring.swap(first)
         moving = project(acts[last][0], down[h], given).astype(BF)
         for r in reversed(range(1, last)):
-            block = after(acts[r][0], first) if h else acts[r][0]
+            block = after(acts[r][0], moving) if h else acts[r][0]
             given = ring.swap(project(block, down[h]).astype(BF))
             came = ring.send(moving)
             moving = project(acts[r][1], down[h], given, came).astype(BF)
@@ -768,9 +812,12 @@
         sums += [project(acts[0][0], down[h], came[tok:]), ring.swap(back)]
 
     lists_in = [pool_ids, list_ids, clicks, ranks, alpha_table[None, :], beta_table[None, :]]
-    *state, totals = score_stage(rolled, sums, head, out_w, lists_in)
+    normed, inv, pooled, head_act, exp_row, corrected, totals = score_stage(
+        rolled, sums, head, out_w, lists_in
+    )
+    slope = slope_stage(normed, inv, head_act, head, out_w, pool_ids, cands)
     list_loss, low, high, packed = grad_stage(
-        totals, across(totals), state, head, out_w, pool_ids, list_ids
+        totals, across(totals), slope, pooled, exp_row, corrected, pool_ids, list_ids
     )
 
     def gather_blocks(x):
@@ -784,7 +831,9 @@
     grads[0] = gather_blocks(low)
     flat = lambda lists: [x for part in lists for x in part]
     act_blocks, slope_blocks = flat(acts), flat(slopes)
-    sent_down = across(outer_sum(act_blocks, grads[1], BF, half))
+    partial = outer_sum(act_blocks[:-3], grads[1][:-3], F32, half)
+    partial = outer_sum(act_blocks[-3:], grads[1][-3:], BF, half, base=partial)
+    sent_down = across(partial)
     split = 2 * (last - 1)
     early = back_stage([grads[0][:split], grads[1][:split]], slope_blocks[:split], down)
     late = back_stage([grads[0][split:], grads[1][split:]], slope_blocks[split:], down)
@@ -794,16 +843,16 @@
         inputs += [mine[r], theirs[r], mine_swapped[r], theirs_swapped[r]]
     inputs += [mine[last], mine_swapped[last]]
     sent_up = across(outer_sum(pre_grads, inputs, BF, half, half, tok))
-    down_local = outer_sum(act_blocks, grads[0], F32, half)
-    up_local = outer_sum(pre_grads, inputs, F32, half, 0, tok)
-
+    down_local = outer_sum(act_blocks, grads[0], BF, half)
+    up_local = outer_sum(pre_grads, inputs, BF, half, 0, tok)
+
+    grad_down = (down_local.astype(F32) + sent_down.astype(F32)).astype(BF).T[None]
     pair = jnp.concatenate([packed, across(packed)])
-    grad_head, grad_out = head_stage(
-        jnp.asarray(ring.table), gather_blocks(pair), head_weight, out_row
-    )
-
-    grad_down = (down_local + sent_down.astype(F32)).astype(BF).T[None]
-    grad_up = (up_local + sent_up.astype(F32)).astype(BF).T[None]
+    blocks = gather_blocks(pair)
+    blocks[0], grad_down = lax.optimization_barrier((blocks[0], grad_down))
+    grad_head, grad_out = head_stage(jnp.asarray(ring.table), blocks, head_weight, out_row)
+
+    grad_up = (up_local.astype(F32) + sent_up.astype(F32)).astype(BF).T[None]
     return (grad_up, grad_down, grad_head, grad_out[0], list_loss[0])
 
 

time: 182 us -> 167 us (0.918)
  waiting for transfers between devices: 89 us -> 70.3 us
  starting transfers between devices: 55.6 us -> 59.7 us
  local copies, waits for them, and re-layouts: 3.63 us -> 1.33 us
  Pallas kernels: 23.6 us -> 25.8 us
    ppermute x27, waiting for transfers between devices: 48.5 us -> 37.4 us  [send(): return lax.ppermute(x, 'expert', self.forward)]
    ppermute x8, waiting for transfers between devices: 38.7 us -> 28.7 us  [across(): return lax.ppermute(x, 'dp', [(0, 1), (1, 0)])]
    ppermute x27, starting transfers between devices: 40.5 us -> 44.1 us  [send(): return lax.ppermute(x, 'expert', self.forward)]
    ppermute x34, waiting for transfers between devices: 1.82 us -> 4.24 us  [swap(): return lax.ppermute(x, 'expert', self.swap_pairs)]
    unnamed x31 -> x27, local copies, waits for them, and re-layouts: 3.6 us -> 1.3 us
    pallas_call x16 -> x18, Pallas kernels: 23.6 us -> 25.8 us  [vmem_call(): pl.pallas_call(kernel, out_shape=outs, in_specs=specs, out_specs=[pl.Bloc...]
    ppermute x8, starting transfers between devices: 9.27 us -> 11.4 us  [across(): return lax.ppermute(x, 'dp', [(0, 1), (1, 0)])]
  transfers between devices with their start and end apart: 69 -> 69, of which waited for: 29 -> 32; matrix products, arithmetic and copies ran while one was open for 4% -> 5% of each run, Pallas kernels for 11% -> 11%
where the time goes in v1:
time: 167 us
  waiting for transfers between devices  70.3 us (42%)
  starting transfers between devices  59.7 us (36%)
  Pallas kernels  25.8 us (15%)
  matrix products  6.59 us (4%)
  other arithmetic  2.14 us (1%)
    ppermute x27, starting transfers between devices, send(): return lax.ppermute(x, 'expert', self.forward)  44.1 us
    ppermute x27, waiting for transfers between devices, send(): return lax.ppermute(x, 'expert', self.forward)  37.4 us
    ppermute x8, waiting for transfers between devices, across(): return lax.ppermute(x, 'dp', [(0, 1), (1, 0)])  28.7 us
    pallas_call x18, Pallas kernels, vmem_call(): pl.pallas_call(kernel, out_shape=outs, in_specs=specs, out_specs=[pl.Bloc...  25.8 us
    ppermute x8, starting transfers between devices, across(): return lax.ppermute(x, 'dp', [(0, 1), (1, 0)])  11.4 us
    dot_general x20, matrix products, project(): total = jnp.dot(act, down, preferred_element_type=F32)  6.59 us
    ppermute x34, waiting for transfers between devices, swap(): return lax.ppermute(x, 'expert', self.swap_pairs)  4.24 us
    ppermute x34, starting transfers between devices, swap(): return lax.ppermute(x, 'expert', self.swap_pairs)  4.21 us
  transfers between devices with their start and end apart: 69, of which 32 were waited for; matrix products, arithmetic and copies ran while one was open for 5% of the time, Pallas kernels for 11%

profile of v1, /device:TPU:0, one launch (start us, length us, event | category | flops | bytes accessed | tf_op | source)
XLA Modules:
  0.0 167.1 jit_solution(4623593005786445981)
XLA Ops:
  0.6 1.8 %shard_map.173.refs_0_.refs_10_ = bf16[136,1024]{1,0:T(8,128)(2,1)} custom-call(bf16[128,1024]{1,0:T(8,128)(2,1)} %tok_hbm.1, s32[4,128]{1,0:T(4,128)} %bitcast.86, f32[4,128]{1,0:T(4,128)} %bitcast.87), custom_call_target="tpu_custom_call" | custom-call | bytes 544768 | tf_op jit(solution)/shard_map/pallas_call | solution.py:279
  3.0 2.6 %collective-permute-start.1 = (bf16[704,512]{1,0:T(8,128)(2,1)}, bf16[704,512]{1,0:T(8,128)(2,1)S(1)}, u32[]{:S(2)}, u32[]{:S(2)}) collective-permute-start(bf16[704,512]{1,0:T(8,128)(2,1)} %bitcast.74), channel_id=1, source_target_pairs={{0,16},{16,0},{1,17},{17,1},{2,18},{18,2},{3,19},{19,3},{4,20},{20... | collective-permute-start | bytes 2162696 | tf_op jit(solution)/shard_map/ppermute | solution.py:766
  8.7 3.6 %collective-permute-done.2.refs_0_.refs_12_ = bf16[136,1024]{1,0:T(8,128)(2,1)S(1)} collective-permute-done((bf16[136,1024]{1,0:T(8,128)(2,1)}, bf16[136,1024]{1,0:T(8,128)(2,1)S(1)}, u32[]{:S(2)}, u32[]{:S(2)}) %collective-permute-start.2) | collective-permute-done | bytes 278560 | tf_op jit(solution)/shard_map/ppermute | solution.py:60
  18.9 3.8 %collective-permute-done.1.refs_3_.refs_5_ = bf16[704,512]{1,0:T(8,128)(2,1)S(1)} collective-permute-done((bf16[704,512]{1,0:T(8,128)(2,1)}, bf16[704,512]{1,0:T(8,128)(2,1)S(1)}, u32[]{:S(2)}, u32[]{:S(2)}) %collective-permute-start.1) | collective-permute-done | bytes 720928 | tf_op jit(solution)/shard_map/ppermute | solution.py:766
  23.9 2.2 %collective-permute-start.12 = (bf16[136,1024]{1,0:T(8,128)(2,1)S(1)}, bf16[136,1024]{1,0:T(8,128)(2,1)S(1)}, u32[]{:S(2)}, u32[]{:S(2)}) collective-permute-start(bf16[136,1024]{1,0:T(8,128)(2,1)S(1)} %collective-permute-done.7.refs_0_.refs_16_), channel_id=1, source_target_pairs={{0,4},{1,3},{4,8},{5,1},{8,12},{9,5},{12,14},{13,9},{14,10},{15,13... | collective-permute-start | bytes 835592 | tf_op jit(solution)/shard_map/ppermute | solution.py:60
  35.1 2.1 %collective-permute-start.37 = (f32[1,512]{1,0:T(1,128)S(1)}, f32[1,512]{1,0:T(1,128)S(1)}, u32[]{:S(2)}, u32[]{:S(2)}) collective-permute-start(f32[1,512]{1,0:T(1,128)S(1)} %bitcast.80), channel_id=1, source_target_pairs={{0,16},{16,0},{1,17},{17,1},{2,18},{18,2},{3,19},{19,3},{4,20},{20... | collective-permute-start | bytes 6152 | tf_op jit(solution)/shard_map/ppermute | solution.py:766
  41.4 7.8 %collective-permute-done.25.refs_19_.refs_13_ = bf16[704,512]{1,0:T(8,128)(2,1)S(1)} collective-permute-done((bf16[704,512]{1,0:T(8,128)(2,1)S(1)}, bf16[704,512]{1,0:T(8,128)(2,1)S(1)}, u32[]{:S(2)}, u32[]{:S(2)}) %collective-permute-start.25) | collective-permute-done | bytes 720928 | tf_op jit(solution)/shard_map/ppermute | solution.py:766
  51.9 1.8 %collective-permute-start.20 = (bf16[128,512]{1,0:T(8,128)(2,1)S(1)}, bf16[128,512]{1,0:T(8,128)(2,1)S(1)}, u32[]{:S(2)}, u32[]{:S(2)}) collective-permute-start(bf16[128,512]{1,0:T(8,128)(2,1)S(1)} %fusion.12), channel_id=1, source_target_pairs={{0,4},{1,3},{4,8},{5,1},{8,12},{9,5},{12,14},{13,9},{14,10},{15,13... | collective-permute-start | bytes 393224 | tf_op jit(solution)/shard_map/ppermute | solution.py:60
  57.2 2.2 %collective-permute-done.28 = bf16[128,512]{1,0:T(8,128)(2,1)S(1)} collective-permute-done((bf16[128,512]{1,0:T(8,128)(2,1)S(1)}, bf16[128,512]{1,0:T(8,128)(2,1)S(1)}, u32[]{:S(2)}, u32[]{:S(2)}) %collective-permute-start.28) | collective-permute-done | bytes 131104 | tf_op jit(solution)/shard_map/ppermute | solution.py:60
  63.4 2.4 %collective-permute-done.21 = bf16[256,512]{1,0:T(8,128)(2,1)S(1)} collective-permute-done((bf16[256,512]{1,0:T(8,128)(2,1)S(1)}, bf16[256,512]{1,0:T(8,128)(2,1)S(1)}, u32[]{:S(2)}, u32[]{:S(2)}) %collective-permute-start.21) | collective-permute-done | bytes 262176 | tf_op jit(solution)/shard_map/ppermute | solution.py:60
  66.2 2.4 %collective-permute-done.30 = bf16[256,512]{1,0:T(8,128)(2,1)S(1)} collective-permute-done((bf16[256,512]{1,0:T(8,128)(2,1)S(1)}, bf16[256,512]{1,0:T(8,128)(2,1)S(1)}, u32[]{:S(2)}, u32[]{:S(2)}) %collective-permute-start.30) | collective-permute-done | bytes 262176 | tf_op jit(solution)/shard_map/ppermute | solution.py:60
  72.6 2.3 %collective-permute-done.22 = bf16[256,512]{1,0:T(8,128)(2,1)S(1)} collective-permute-done((bf16[256,512]{1,0:T(8,128)(2,1)S(1)}, bf16[256,512]{1,0:T(8,128)(2,1)S(1)}, u32[]{:S(2)}, u32[]{:S(2)}) %collective-permute-start.22) | collective-permute-done | bytes 262176 | tf_op jit(solution)/shard_map/ppermute | solution.py:60
  78.1 1.8 %collective-permute-start.33 = (bf16[256,512]{1,0:T(8,128)(2,1)S(1)}, bf16[256,512]{1,0:T(8,128)(2,1)S(1)}, u32[]{:S(2)}, u32[]{:S(2)}) collective-permute-start(bf16[256,512]{1,0:T(8,128)(2,1)S(1)} %fusion.9), channel_id=1, source_target_pairs={{0,4},{1,3},{4,8},{5,1},{8,12},{9,5},{12,14},{13,9},{14,10},{15,13... | collective-permute-start | bytes 786440 | tf_op jit(solution)/shard_map/ppermute | solution.py:60
  80.0 1.8 %collective-permute-done.23 = bf16[256,512]{1,0:T(8,128)(2,1)S(1)} collective-permute-done((bf16[256,512]{1,0:T(8,128)(2,1)S(1)}, bf16[256,512]{1,0:T(8,128)(2,1)S(1)}, u32[]{:S(2)}, u32[]{:S(2)}) %collective-permute-start.23) | collective-permute-done | bytes 262176 | tf_op jit(solution)/shard_map/ppermute | solution.py:60
  82.5 2.3 %collective-permute-done.33 = bf16[256,512]{1,0:T(8,128)(2,1)S(1)} collective-permute-done((bf16[256,512]{1,0:T(8,128)(2,1)S(1)}, bf16[256,512]{1,0:T(8,128)(2,1)S(1)}, u32[]{:S(2)}, u32[]{:S(2)}) %collective-permute-start.33) | collective-permute-done | bytes 262176 | tf_op jit(solution)/shard_map/ppermute | solution.py:60
  96.9 3.1 %collective-permute-done.40.refs_2_.refs_12_ = bf16[256,512]{1,0:T(8,128)(2,1)S(1)} collective-permute-done((bf16[256,512]{1,0:T(8,128)(2,1)S(1)}, bf16[256,512]{1,0:T(8,128)(2,1)S(1)}, u32[]{:S(2)}, u32[]{:S(2)}) %collective-permute-start.40) | collective-permute-done | bytes 262176 | tf_op jit(solution)/shard_map/ppermute | solution.py:60
  110.8 2.0 %collective-permute-done.49.refs_0_.refs_16_ = bf16[256,512]{1,0:T(8,128)(2,1)S(1)} collective-permute-done((bf16[256,512]{1,0:T(8,128)(2,1)S(1)}, bf16[256,512]{1,0:T(8,128)(2,1)S(1)}, u32[]{:S(2)}, u32[]{:S(2)}) %collective-permute-start.49) | collective-permute-done | bytes 262176 | tf_op jit(solution)/shard_map/ppermute | solution.py:60
  112.8 2.8 %collective-permute-done.53.refs_4_.refs_13_ = bf16[256,512]{1,0:T(8,128)(2,1)S(1)} collective-permute-done((bf16[256,512]{1,0:T(8,128)(2,1)S(1)}, bf16[256,512]{1,0:T(8,128)(2,1)S(1)}, u32[]{:S(2)}, u32[]{:S(2)}) %collective-permute-start.53) | collective-permute-done | bytes 262176 | tf_op jit(solution)/shard_map/ppermute | solution.py:60
  122.2 2.6 %shard_map.183 = (bf16[128,704]{1,0:T(8,128)(2,1)S(1)}, bf16[128,704]{1,0:T(8,128)(2,1)S(1)}, bf16[256,704]{1,0:T(8,128)(2,1)S(1)}, bf16[256,704]{1,0:T(8,128)(2...) custom-call(bf16[128,512]{1,0:T(8,128)(2,1)S(1)} %get-tuple-element.73.refs_0_.refs_10_, ...), custom_call_target="tpu_custom_call" | custom-call | flops 1845493760 | bytes 7667712 | tf_op jit(solution)/shard_map/pallas_call | solution.py:279
  124.9 1.8 %shard_map.184 = (bf16[256,704]{1,0:T(8,128)(2,1)S(1)}, bf16[256,704]{1,0:T(8,128)(2,1)S(1)}, bf16[128,704]{1,0:T(8,128)(2,1)S(1)}, bf16[128,704]{1,0:T(8,128)(2,1)S(1)}) custom-call(bf16[256,512]{1,0:T(8,128)(2,1)S(1)} %collective-permute-done.49.refs_0_.refs_16_, bf16[256,512]{1,0:T(8,128)(2,1)S(1)} %collective-permute-done.50.refs_1_.refs_17_, ...), custom_call_target="tpu_custom_call" | custom-call | flops 1107296256 | bytes 5177344 | tf_op jit(solution)/shard_map/pallas_call | solution.py:279
  137.3 3.1 %collective-permute-done.65.refs_6_ = bf16[64,1152]{1,0:T(8,128)(2,1)S(1)} collective-permute-done((bf16[64,1152]{1,0:T(8,128)(2,1)S(1)}, bf16[64,1152]{1,0:T(8,128)(2,1)S(1)}, u32[]{:S(2)}, u32[]{:S(2)}) %collective-permute-start.65) | collective-permute-done | bytes 147488 | tf_op jit(solution)/shard_map/ppermute | solution.py:60
  145.5 2.1 %collective-permute-done.57 = bf16[704,512]{1,0:T(8,128)(2,1)S(1)} collective-permute-done((bf16[704,512]{1,0:T(8,128)(2,1)S(1)}, bf16[704,512]{1,0:T(8,128)(2,1)S(1)}, u32[]{:S(2)}, u32[]{:S(2)}) %collective-permute-start.57) | collective-permute-done | bytes 720928 | tf_op jit(solution)/shard_map/ppermute | solution.py:766
  148.6 13.9 %collective-permute-done.59 = bf16[704,512]{1,0:T(8,128)(2,1)S(1)} collective-permute-done((bf16[704,512]{1,0:T(8,128)(2,1)S(1)}, bf16[704,512]{1,0:T(8,128)(2,1)S(1)}, u32[]{:S(2)}, u32[]{:S(2)}) %collective-permute-start.59) | collective-permute-done | bytes 720928 | tf_op jit(solution)/shard_map/ppermute | solution.py:766
  163.6 3.5 %shard_map.190 = (f32[512,1024]{1,0:T(8,128)}, f32[1,512]{1,0:T(1,128)}) custom-call(s32[16,16]{1,0:T(8,128)S(1)} %copy-done.12, bf16[32,1152]{1,0:T(8,128)(2,1)S(1)} %constant_dynamic-update-slice_fusion.refs_0_, bf16[32,1152]{1,0:T(8,128)(2,1)S(1)} %collective-permute-done.60.refs_1_, bf16[64,1152]{1,0:T(8,128)(2,1)S(1)} %collective-permute-done.61.refs_2_, ...), custom_call_target="tpu_custom_call" | custom-call | flops 1073741824 | bytes 4330496 | tf_op jit(solution)/shard_map/pallas_call | solution.py:279
  (188 shorter events, 90.1 us)
Async XLA Ops:
  3.0 19.8 %collective-permute-start.1 = (bf16[704,512]{1,0:T(8,128)(2,1)}, bf16[704,512]{1,0:T(8,128)(2,1)S(1)}, u32[]{:S(2)}, u32[]{:S(2)}) collective-permute-start(bf16[704,512]{1,0:T(8,128)(2,1)} %bitcast.74), channel_id=1, source_target_pairs={{0,16},{16,0},{1,17},{17,1},{2,18},{18,2},{3,19},{19,3},{4,20},{20... | collective-permute-start | bytes 2162696 | tf_op jit(solution)/shard_map/ppermute | solution.py:766
  7.1 8.2 %collective-permute-start.3 = (bf16[136,1024]{1,0:T(8,128)(2,1)S(1)}, bf16[136,1024]{1,0:T(8,128)(2,1)S(1)}, u32[]{:S(2)}, u32[]{:S(2)}) collective-permute-start(bf16[136,1024]{1,0:T(8,128)(2,1)S(1)} %collective-permute-done.refs_1_.refs_11_), channel_id=1, source_target_pairs={{0,4},{1,3},{4,8},{5,1},{8,12},{9,5},{12,14},{13,9},{14,10},{15,13... | collective-permute-start | bytes 835592 | tf_op jit(solution)/shard_map/ppermute | solution.py:60
  13.9 10.0 %collective-permute-start.4 = (bf16[136,1024]{1,0:T(8,128)(2,1)S(1)}, bf16[136,1024]{1,0:T(8,128)(2,1)S(1)}, u32[]{:S(2)}, u32[]{:S(2)}) collective-permute-start(bf16[136,1024]{1,0:T(8,128)(2,1)S(1)} %collective-permute-done.2.refs_0_.refs_12_), channel_id=1, source_target_pairs={{0,1},{1,0},{2,3},{3,2},{4,5},{5,4},{6,7},{7,6},{8,9},{9,8},{10,11... | collective-permute-start | bytes 835592 | tf_op jit(solution)/shard_map/ppermute | solution.py:63
  15.3 10.7 %collective-permute-start.8 = (bf16[136,1024]{1,0:T(8,128)(2,1)S(1)}, bf16[136,1024]{1,0:T(8,128)(2,1)S(1)}, u32[]{:S(2)}, u32[]{:S(2)}) collective-permute-start(bf16[136,1024]{1,0:T(8,128)(2,1)S(1)} %collective-permute-done.3.refs_1_.refs_13_), channel_id=1, source_target_pairs={{0,4},{1,3},{4,8},{5,1},{8,12},{9,5},{12,14},{13,9},{14,10},{15,13... | collective-permute-start | bytes 835592 | tf_op jit(solution)/shard_map/ppermute | solution.py:60
  16.9 9.3 %collective-permute-start.5 = (bf16[136,1024]{1,0:T(8,128)(2,1)S(1)}, bf16[136,1024]{1,0:T(8,128)(2,1)S(1)}, u32[]{:S(2)}, u32[]{:S(2)}) collective-permute-start(bf16[136,1024]{1,0:T(8,128)(2,1)S(1)} %collective-permute-done.3.refs_1_.refs_13_), channel_id=1, source_target_pairs={{0,1},{1,0},{2,3},{3,2},{4,5},{5,4},{6,7},{7,6},{8,9},{9,8},{10,11... | collective-permute-start | bytes 835592 | tf_op jit(solution)/shard_map/ppermute | solution.py:63
  18.8 16.2 %collective-permute-start.35 = (bf16[256,1024]{1,0:T(8,128)(2,1)S(1)}, bf16[256,1024]{1,0:T(8,128)(2,1)S(1)}, u32[]{:S(2)}, u32[]{:S(2)}) collective-permute-start(bf16[256,1024]{1,0:T(8,128)(2,1)S(1)} %shard_map.179), channel_id=1, source_target_pairs={{0,16},{16,0},{1,17},{17,1},{2,18},{18,2},{3,19},{19,3},{4,20},{20... | collective-permute-start | bytes 1572872 | tf_op jit(solution)/shard_map/ppermute | solution.py:766
  26.2 7.3 %collective-permute-start.13 = (bf16[136,1024]{1,0:T(8,128)(2,1)S(1)}, bf16[136,1024]{1,0:T(8,128)(2,1)S(1)}, u32[]{:S(2)}, u32[]{:S(2)}) collective-permute-start(bf16[136,1024]{1,0:T(8,128)(2,1)S(1)} %collective-permute-done.8.refs_1_.refs_17_), channel_id=1, source_target_pairs={{0,4},{1,3},{4,8},{5,1},{8,12},{9,5},{12,14},{13,9},{14,10},{15,13... | collective-permute-start | bytes 835592 | tf_op jit(solution)/shard_map/ppermute | solution.py:60
  29.3 19.9 %collective-permute-start.25 = (bf16[704,512]{1,0:T(8,128)(2,1)S(1)}, bf16[704,512]{1,0:T(8,128)(2,1)S(1)}, u32[]{:S(2)}, u32[]{:S(2)}) collective-permute-start(bf16[704,512]{1,0:T(8,128)(2,1)S(1)} %bitcast.71), channel_id=1, source_target_pairs={{0,16},{16,0},{1,17},{17,1},{2,18},{18,2},{3,19},{19,3},{4,20},{20... | collective-permute-start | bytes 2162696 | tf_op jit(solution)/shard_map/ppermute | solution.py:766
  35.1 50.3 %collective-permute-start.37 = (f32[1,512]{1,0:T(1,128)S(1)}, f32[1,512]{1,0:T(1,128)S(1)}, u32[]{:S(2)}, u32[]{:S(2)}) collective-permute-start(f32[1,512]{1,0:T(1,128)S(1)} %bitcast.80), channel_id=1, source_target_pairs={{0,16},{16,0},{1,17},{17,1},{2,18},{18,2},{3,19},{19,3},{4,20},{20... | collective-permute-start | bytes 6152 | tf_op jit(solution)/shard_map/ppermute | solution.py:766
  37.1 48.3 %collective-permute-start.36 = (bf16[256,1024]{1,0:T(8,128)(2,1)S(1)}, bf16[256,1024]{1,0:T(8,128)(2,1)S(1)}, u32[]{:S(2)}, u32[]{:S(2)}) collective-permute-start(bf16[256,1024]{1,0:T(8,128)(2,1)S(1)} %collective-permute-done.35.refs_6_.refs_1_), channel_id=1, source_target_pairs={{0,1},{1,0},{2,3},{3,2},{4,5},{5,4},{6,7},{7,6},{8,9},{9,8},{10,11... | collective-permute-start | bytes 1572872 | tf_op jit(solution)/shard_map/ppermute | solution.py:63
  37.4 35.1 %collective-permute-start.6 = (bf16[256,512]{1,0:T(8,128)(2,1)S(1)}, bf16[256,512]{1,0:T(8,128)(2,1)S(1)}, u32[]{:S(2)}, u32[]{:S(2)}) collective-permute-start(bf16[256,512]{1,0:T(8,128)(2,1)S(1)} %convolution_convert_fusion.5), channel_id=1, source_target_pairs={{0,1},{1,0},{2,3},{3,2},{4,5},{5,4},{6,7},{7,6},{8,9},{9,8},{10,11... | collective-permute-start | bytes 786440 | tf_op jit(solution)/shard_map/ppermute | solution.py:63
  39.8 14.6 %collective-permute-start.16 = (bf16[256,512]{1,0:T(8,128)(2,1)S(1)}, bf16[256,512]{1,0:T(8,128)(2,1)S(1)}, u32[]{:S(2)}, u32[]{:S(2)}) collective-permute-start(bf16[256,512]{1,0:T(8,128)(2,1)S(1)} %convolution_convert_fusion.3), channel_id=1, source_target_pairs={{0,1},{1,0},{2,3},{3,2},{4,5},{5,4},{6,7},{7,6},{8,9},{9,8},{10,11... | collective-permute-start | bytes 786440 | tf_op jit(solution)/shard_map/ppermute | solution.py:63
  70.5 7.2 %collective-permute-start.32 = (bf16[256,512]{1,0:T(8,128)(2,1)S(1)}, bf16[256,512]{1,0:T(8,128)(2,1)S(1)}, u32[]{:S(2)}, u32[]{:S(2)}) collective-permute-start(bf16[256,512]{1,0:T(8,128)(2,1)S(1)} %fusion.10), channel_id=1, source_target_pairs={{0,4},{1,3},{4,8},{5,1},{8,12},{9,5},{12,14},{13,9},{14,10},{15,13... | collective-permute-start | bytes 786440 | tf_op jit(solution)/shard_map/ppermute | solution.py:60
  95.3 7.6 %collective-permute-start.45 = (bf16[256,512]{1,0:T(8,128)(2,1)S(1)}, bf16[256,512]{1,0:T(8,128)(2,1)S(1)}, u32[]{:S(2)}, u32[]{:S(2)}) collective-permute-start(bf16[256,512]{1,0:T(8,128)(2,1)S(1)} %pad_maximum_fusion.1), channel_id=1, source_target_pairs={{0,4},{1,3},{4,8},{5,1},{8,12},{9,5},{12,14},{13,9},{14,10},{15,13... | collective-permute-start | bytes 786440 | tf_op jit(solution)/shard_map/ppermute | solution.py:60
  108.0 9.3 %collective-permute-start.41 = (bf16[256,512]{1,0:T(8,128)(2,1)S(1)}, bf16[256,512]{1,0:T(8,128)(2,1)S(1)}, u32[]{:S(2)}, u32[]{:S(2)}) collective-permute-start(bf16[256,512]{1,0:T(8,128)(2,1)S(1)} %collective-permute-done.40.refs_2_.refs_12_), channel_id=1, source_target_pairs={{0,1},{1,0},{2,3},{3,2},{4,5},{5,4},{6,7},{7,6},{8,9},{9,8},{10,11... | collective-permute-start | bytes 786440 | tf_op jit(solution)/shard_map/ppermute | solution.py:63
  108.0 10.9 %collective-permute-start.46 = (bf16[256,512]{1,0:T(8,128)(2,1)S(1)}, bf16[256,512]{1,0:T(8,128)(2,1)S(1)}, u32[]{:S(2)}, u32[]{:S(2)}) collective-permute-start(bf16[256,512]{1,0:T(8,128)(2,1)S(1)} %collective-permute-done.45.refs_8_.refs_9_), channel_id=1, source_target_pairs={{0,1},{1,0},{2,3},{3,2},{4,5},{5,4},{6,7},{7,6},{8,9},{9,8},{10,11... | collective-permute-start | bytes 786440 | tf_op jit(solution)/shard_map/ppermute | solution.py:63
  108.5 10.4 %collective-permute-start.43 = (bf16[256,512]{1,0:T(8,128)(2,1)S(1)}, bf16[256,512]{1,0:T(8,128)(2,1)S(1)}, u32[]{:S(2)}, u32[]{:S(2)}) collective-permute-start(bf16[256,512]{1,0:T(8,128)(2,1)S(1)} %collective-permute-done.42.refs_4_.refs_14_), channel_id=1, source_target_pairs={{0,1},{1,0},{2,3},{3,2},{4,5},{5,4},{6,7},{7,6},{8,9},{9,8},{10,11... | collective-permute-start | bytes 786440 | tf_op jit(solution)/shard_map/ppermute | solution.py:63
  119.4 10.6 %collective-permute-start.61 = (bf16[64,1152]{1,0:T(8,128)(2,1)S(1)}, bf16[64,1152]{1,0:T(8,128)(2,1)S(1)}, u32[]{:S(2)}, u32[]{:S(2)}) collective-permute-start(bf16[64,1152]{1,0:T(8,128)(2,1)S(1)} %pad_maximum_fusion.2), channel_id=1, source_target_pairs={{0,4},{1,3},{4,8},{5,1},{8,12},{9,5},{12,14},{13,9},{14,10},{15,13... | collective-permute-start | bytes 442376 | tf_op jit(solution)/shard_map/ppermute | solution.py:60
  128.5 19.1 %collective-permute-start.57 = (bf16[704,512]{1,0:T(8,128)(2,1)S(1)}, bf16[704,512]{1,0:T(8,128)(2,1)S(1)}, u32[]{:S(2)}, u32[]{:S(2)}) collective-permute-start(bf16[704,512]{1,0:T(8,128)(2,1)S(1)} %shard_map.186), channel_id=1, source_target_pairs={{0,16},{16,0},{1,17},{17,1},{2,18},{18,2},{3,19},{19,3},{4,20},{20... | collective-permute-start | bytes 2162696 | tf_op jit(solution)/shard_map/ppermute | solution.py:766
  133.5 29.0 %collective-permute-start.59 = (bf16[704,512]{1,0:T(8,128)(2,1)S(1)}, bf16[704,512]{1,0:T(8,128)(2,1)S(1)}, u32[]{:S(2)}, u32[]{:S(2)}) collective-permute-start(bf16[704,512]{1,0:T(8,128)(2,1)S(1)} %shard_map.189), channel_id=1, source_target_pairs={{0,16},{16,0},{1,17},{17,1},{2,18},{18,2},{3,19},{19,3},{4,20},{20... | collective-permute-start | bytes 2162696 | tf_op jit(solution)/shard_map/ppermute | solution.py:766
  136.8 26.8 %collective-permute-start.62 = (bf16[64,1152]{1,0:T(8,128)(2,1)S(1)}, bf16[64,1152]{1,0:T(8,128)(2,1)S(1)}, u32[]{:S(2)}, u32[]{:S(2)}) collective-permute-start(bf16[64,1152]{1,0:T(8,128)(2,1)S(1)} %collective-permute-done.61.refs_2_), channel_id=1, source_target_pairs={{0,1},{1,0},{2,3},{3,2},{4,5},{5,4},{6,7},{7,6},{8,9},{9,8},{10,11... | collective-permute-start | bytes 442376 | tf_op jit(solution)/shard_map/ppermute | solution.py:63
  136.8 26.8 %collective-permute-start.64 = (bf16[64,1152]{1,0:T(8,128)(2,1)S(1)}, bf16[64,1152]{1,0:T(8,128)(2,1)S(1)}, u32[]{:S(2)}, u32[]{:S(2)}) collective-permute-start(bf16[64,1152]{1,0:T(8,128)(2,1)S(1)} %collective-permute-done.63.refs_4_), channel_id=1, source_target_pairs={{0,1},{1,0},{2,3},{3,2},{4,5},{5,4},{6,7},{7,6},{8,9},{9,8},{10,11... | collective-permute-start | bytes 442376 | tf_op jit(solution)/shard_map/ppermute | solution.py:63
  145.4 18.2 %collective-permute-start.66 = (bf16[64,1152]{1,0:T(8,128)(2,1)S(1)}, bf16[64,1152]{1,0:T(8,128)(2,1)S(1)}, u32[]{:S(2)}, u32[]{:S(2)}) collective-permute-start(bf16[64,1152]{1,0:T(8,128)(2,1)S(1)} %collective-permute-done.65.refs_6_), channel_id=1, source_target_pairs={{0,1},{1,0},{2,3},{3,2},{4,5},{5,4},{6,7},{7,6},{8,9},{9,8},{10,11... | collective-permute-start | bytes 442376 | tf_op jit(solution)/shard_map/ppermute | solution.py:63
  147.6 16.0 %collective-permute-start.68 = (bf16[32,1152]{1,0:T(8,128)(2,1)S(1)}, bf16[32,1152]{1,0:T(8,128)(2,1)S(1)}, u32[]{:S(2)}, u32[]{:S(2)}) collective-permute-start(bf16[32,1152]{1,0:T(8,128)(2,1)S(1)} %collective-permute-done.67.refs_8_), channel_id=1, source_target_pairs={{0,1},{1,0},{2,3},{3,2},{4,5},{5,4},{6,7},{7,6},{8,9},{9,8},{10,11... | collective-permute-start | bytes 221192 | tf_op jit(solution)/shard_map/ppermute | solution.py:63
  (58 other events, 279.6 us)

commit v2 on v1

--- a/solution.py
+++ b/solution.py
@@ -6,6 +6,8 @@
 from jax.experimental.pallas import tpu as pltpu
 from jax.sharding import PartitionSpec as P
 
+EXPERT = "expert"
+DP = "dp"
 LISTS = 8
 RANKS = 32
 BF = jnp.bfloat16
@@ -57,10 +59,10 @@
         self.table = table
 
     def send(self, x):
-        return lax.ppermute(x, "expert", self.forward)
+        return lax.ppermute(x, EXPERT, self.forward)
 
     def swap(self, x):
-        return lax.ppermute(x, "expert", self.swap_pairs)
+        return lax.ppermute(x, EXPERT, self.swap_pairs)
 
     def gather(self, x):
         rows = x.shape[0]
@@ -97,7 +99,7 @@
     tok_count = tokens.shape[0]
     model_width = tokens.shape[1]
     top_count = route_ids.shape[1]
-    owners = lax.axis_size("expert")
+    owners = lax.axis_size(EXPERT)
     capacity = 3 * tok_count * top_count // (2 * owners)
     slot_total = owners * capacity
     flat_ids = route_ids.reshape(-1)
@@ -113,7 +115,7 @@
     )
     received = lax.all_to_all(
         outgoing.reshape(owners, capacity, model_width),
-        "expert",
+        EXPERT,
         split_axis=0,
         concat_axis=0,
         tiled=True,
@@ -125,19 +127,19 @@
     columns = inputs
     pre_act = jnp.dot(
         columns,
-        lax.all_gather(up_local, "dp", axis=0, tiled=True),
+        lax.all_gather(up_local, DP, axis=0, tiled=True),
         preferred_element_type=jnp.float32,
     )
     activated = jax.nn.silu(pre_act).astype(jnp.bfloat16)
     expert_out = lax.dot_general(
         activated,
-        lax.all_gather(down_local, "dp", axis=0, tiled=True),
+        lax.all_gather(down_local, DP, axis=0, tiled=True),
         (((1,), (1,)), ((), ())),
         preferred_element_type=jnp.float32,
     ).astype(jnp.bfloat16)
     returned = lax.all_to_all(
         expert_out.reshape(owners, capacity, model_width),
-        "expert",
+        EXPERT,
         split_axis=0,
         concat_axis=0,
         tiled=True,
@@ -160,7 +162,7 @@
         preferred_element_type=jnp.float32,
     )
     pooled = (pooled_sum / token_counts[:, None]).astype(jnp.bfloat16)
-    all_pooled = lax.all_gather(pooled, "dp", axis=0, tiled=True)
+    all_pooled = lax.all_gather(pooled, DP, axis=0, tiled=True)
     head_act = jnp.tanh(
         lax.dot_general(
             all_pooled, head_weight, (((1,), (1,)), ((), ())), preferred_element_type=jnp.float32
@@ -177,10 +179,10 @@
         jnp.float32
     )
     group_corrected, group_lists = (
-        lax.all_gather(corrected, "dp", axis=0, tiled=True),
-        lax.all_gather(list_hot, "dp", axis=0, tiled=True),
-    )
-    group_scores = lax.psum(part_score, "dp")
+        lax.all_gather(corrected, DP, axis=0, tiled=True),
+        lax.all_gather(list_hot, DP, axis=0, tiled=True),
+    )
+    group_scores = lax.psum(part_score, DP)
     exp_scores = jnp.exp(group_scores)
     exp_total = jnp.sum(exp_scores[:, None] * group_lists, axis=0)
     click_total = jnp.sum(group_corrected[:, None] * group_lists, axis=0)
@@ -198,12 +200,12 @@
     )
     out_term = jnp.sum(group_grad[:, None] * head_act, axis=0)
     grad_head, grad_out = (
-        lax.psum(head_term.astype(jnp.bfloat16), "expert").astype(jnp.float32),
-        lax.psum(out_term.astype(jnp.bfloat16), "expert").astype(jnp.float32),
+        lax.psum(head_term.astype(jnp.bfloat16), EXPERT).astype(jnp.float32),
+        lax.psum(out_term.astype(jnp.bfloat16), EXPERT).astype(jnp.float32),
     )
     pooled_grad = lax.psum_scatter(
         jnp.dot(hid_grad, head_weight, preferred_element_type=jnp.float32).astype(jnp.bfloat16),
-        "dp",
+        DP,
         scatter_dimension=0,
         tiled=True,
     ).astype(jnp.float32)
@@ -224,7 +226,7 @@
     outgoing_grad = jnp.zeros((slot_total, model_width), jnp.bfloat16).at[target].set(cotangent)
     slot_grad = lax.all_to_all(
         outgoing_grad.reshape(owners, capacity, model_width),
-        "expert",
+        EXPERT,
         split_axis=0,
         concat_axis=0,
         tiled=True,
@@ -232,7 +234,7 @@
     columns = slot_grad
     act_grad = jnp.dot(
         columns,
-        lax.all_gather(down_local, "dp", axis=0, tiled=True),
+        lax.all_gather(down_local, DP, axis=0, tiled=True),
         preferred_element_type=jnp.float32,
     )
     pre_grad = (act_grad * silu_slope(pre_act)).astype(jnp.bfloat16)
@@ -244,7 +246,7 @@
     )
     summed = lax.psum_scatter(
         jnp.concatenate([up_term, down_term], axis=1).astype(jnp.bfloat16),
-        "dp",
+        DP,
         scatter_dimension=0,
         tiled=True,
     ).astype(jnp.float32)
@@ -322,7 +324,7 @@
             pull.start()
         for pull in pulls:
             pull.wait()
-        swapped = lax.axis_index("dp") != 0
+        swapped = lax.axis_index(DP) != 0
         out_ref[:tok, :half] = jnp.where(swapped, tok_ref[:, half:], tok_ref[:, :half])
         out_ref[:tok, half:] = jnp.where(swapped, tok_ref[:, :half], tok_ref[:, half:])
         lanes = [[] for _ in range(extra)]
@@ -391,7 +393,7 @@
             pre = dot_rows(x[:, :half], up0[...]) + dot_rows(x[:, half:], up1[...])
             sig = 1.0 / (1.0 + jnp.exp(-pre))
             for b in range(g):
-                w = weight_column(xs[j], tok, owners, lax.axis_index("expert"))
+                w = weight_column(xs[j], tok, owners, lax.axis_index(EXPERT))
                 p = pre[b * tok : (b + 1) * tok]
                 s = sig[b * tok : (b + 1) * tok]
                 ws = w * s
@@ -507,13 +509,6 @@
     return (lax.broadcasted_iota(jnp.int32, (cands, row.shape[1]), 0) == row).astype(F32)
 
 
-def units_of(head_refs, own_ref, other_ref):
-    part = head_refs[1].shape[0]
-    first = lax.axis_index("expert") % 2 == 0
-    low, high = other_ref[:, :part], other_ref[:, part:]
-    return [own_ref[...], jnp.where(first, low, high), jnp.where(first, high, low)]
-
-
 def score_stage(rolled, sums, head, out_w, lists_in):
     width = rolled.shape[1]
     tok = sums[0].shape[0]
@@ -526,9 +521,9 @@
         rolled_ref = refs[0]
         sum_refs = refs[1 : 1 + 2 * per_half]
         rest = refs[1 + 2 * per_half :]
-        head_refs, out_refs = rest[:3], rest[3:5]
-        pool_ref, list_ref, click_ref, rank_ref, alpha_ref, beta_ref = rest[5:11]
-        normed_ref, inv_ref, pooled_ref, act_ref, exp_ref, corr_ref, tot_ref = rest[11:]
+        head_refs, out_refs = rest[:2], rest[2:4]
+        pool_ref, list_ref, click_ref, rank_ref, alpha_ref, beta_ref = rest[4:10]
+        normed_ref, inv_ref, pooled_ref, act_ref, exp_ref, corr_ref, tot_ref = rest[10:]
         mixed = []
         for h in range(2):
             value = rolled_ref[:tok, h * half : (h + 1) * half].astype(F32)
@@ -550,17 +545,17 @@
                 )
                 / counts
             )
-        swapped = lax.axis_index("dp") != 0
+        swapped = lax.axis_index(DP) != 0
         pooled_ref[:, :half] = jnp.where(swapped, pooled[1], pooled[0]).astype(BF)
         pooled_ref[:, half:] = jnp.where(swapped, pooled[0], pooled[1]).astype(BF)
         both = pooled_ref[...]
         scores = jnp.zeros((cands, 1), F32)
         at = 0
-        for head_ref, out_row in zip(head_refs, units_of(head_refs, *out_refs)):
+        for head_ref, out_row in zip(head_refs, out_refs):
             size = head_ref.shape[0]
             act = jnp.tanh(dot_rows(both, head_ref[...]))
             act_ref[:, at : at + size] = act
-            scores = scores + jnp.sum(act * out_row, axis=1, keepdims=True)
+            scores = scores + jnp.sum(act * out_row[...], axis=1, keepdims=True)
             at += size
         score_row = to_row(scores)
         exp_row = jnp.exp(score_row)
@@ -595,18 +590,18 @@
     half = width // 2
 
     def kernel(normed_ref, inv_ref, act_ref, *refs):
-        head_refs, out_refs, pool_ref, slope_ref = refs[:3], refs[3:5], refs[5], refs[6]
+        head_refs, out_refs, pool_ref, slope_ref = refs[:2], refs[2:4], refs[4], refs[5]
         back = jnp.zeros((cands, width), F32)
         at = 0
-        for head_ref, out_row in zip(head_refs, units_of(head_refs, *out_refs)):
+        for head_ref, out_row in zip(head_refs, out_refs):
             size = head_ref.shape[0]
             act = act_ref[:, at : at + size]
-            hid = (out_row * (1.0 - act * act)).astype(BF)
+            hid = (out_row[...] * (1.0 - act * act)).astype(BF)
             back = back + jnp.dot(hid, head_ref[...], preferred_element_type=F32)
             at += size
         hot = pool_of(pool_ref, cands)
         back = back / jnp.sum(hot, axis=1, keepdims=True)
-        swapped = lax.axis_index("dp") != 0
+        swapped = lax.axis_index(DP) != 0
         parts = [
             jnp.where(swapped, back[:, half:], back[:, :half]),
             jnp.where(swapped, back[:, :half], back[:, half:]),
@@ -692,7 +687,7 @@
     def kernel(table_ref, *refs):
         block_refs = refs[:count]
         head_ref, out_ref, grad_ref, out_grad_ref, buffer = refs[count:]
-        mine, plane = lax.axis_index("expert"), lax.axis_index("dp")
+        mine, plane = lax.axis_index(EXPERT), lax.axis_index(DP)
         j = 0
         for ref in block_refs:
             for piece in range(ref.shape[0] // each):
@@ -722,16 +717,6 @@
     )
 
 
-def pick_half(head):
-    rows = head.shape[0] // 2
-
-    def kernel(head_ref, out_ref):
-        first = lax.axis_index("expert") % 2 == 0
-        out_ref[...] = jnp.where(first, head_ref[:rows, :], head_ref[rows:, :])
-
-    return vmem_call(kernel, [shaped((rows, head.shape[1]), head.dtype)], [head])[0]
-
-
 def after(value, *others):
     return lax.optimization_barrier((value,) + others)[0]
 
@@ -755,7 +740,7 @@
     alpha_table,
     beta_table,
 ):
-    n_exp = lax.axis_size("expert")
+    n_exp = lax.axis_size(EXPERT)
     ring = Ring(n_exp)
     last = ring.half
     tok, width = tokens.shape
@@ -763,7 +748,7 @@
     cands = list_ids.shape[1]
 
     def across(x):
-        return lax.ppermute(x, "dp", [(0, 1), (1, 0)])
+        return lax.ppermute(x, DP, [(0, 1), (1, 0)])
 
     up_own, down_own = up_weight[0].T, down_weight[0].T
     up = [up_own, across(up_own)]
@@ -779,8 +764,7 @@
             theirs_swapped.append(ring.swap(theirs[-1]))
 
     down = [down_own, across(down_own)]
-    head_came = across(pick_half(head_weight))
-    head = [head_weight, head_came, ring.swap(head_came)]
+    head = [head_weight, across(head_weight)]
     out_row = out_weight[None, :]
     out_w = [out_row, across(out_row)]
 
@@ -857,31 +841,31 @@
 
 
 def solution(mesh):
-    paired = mesh.shape["dp"] == 2 and mesh.shape["expert"] % 4 == 0
+    paired = mesh.shape[DP] == 2 and mesh.shape[EXPERT] % 4 == 0
     return jax.shard_map(
         dense_local if paired else routed_local,
         mesh=mesh,
         in_specs=(
-            P(("dp", "expert"), None),
-            P(("dp", "expert"), None),
-            P(("dp", "expert"), None),
-            P("expert", "dp", None),
-            P("expert", "dp", None),
-            P("dp", None),
-            P("dp"),
-            P(("dp", "expert"), None),
-            P(("dp", "expert"), None),
-            P(("dp", "expert"), None),
-            P(("dp", "expert"), None),
+            P((DP, EXPERT), None),
+            P((DP, EXPERT), None),
+            P((DP, EXPERT), None),
+            P(EXPERT, DP, None),
+            P(EXPERT, DP, None),
+            P(DP, None),
+            P(DP),
+            P((DP, EXPERT), None),
+            P((DP, EXPERT), None),
+            P((DP, EXPERT), None),
+            P((DP, EXPERT), None),
             P(),
             P(),
         ),
         out_specs=(
-            P("expert", "dp", None),
-            P("expert", "dp", None),
-            P("dp", None),
-            P("dp"),
-            P("expert"),
+            P(EXPERT, DP, None),
+            P(EXPERT, DP, None),
+            P(DP, None),
+            P(DP),
+            P(EXPERT),
         ),
         check_vma=False,
     )

time: 167 us -> 161 us (0.964)
  waiting for transfers between devices: 70.3 us -> 63.3 us
    ppermute x69 -> x68, waiting for transfers between devices: 70.3 us -> 63.3 us  [the longest x27 39 us: send(): return lax.ppermute(x, EXPERT, self.forward)]
    ppermute x69 -> x68, starting transfers between devices: 59.7 us -> 59.8 us  [the longest x27 43.8 us: send(): return lax.ppermute(x, EXPERT, self.forward)]
    pallas_call x18 -> x17, Pallas kernels: 25.8 us -> 25.7 us  [vmem_call(): pl.pallas_call(kernel, out_shape=outs, in_specs=specs, out_specs=[pl.Bloc...]
  transfers between devices with their start and end apart: 69 -> 68, of which waited for: 32 -> 30; matrix products, arithmetic and copies ran while one was open for 5% -> 5% of each run, Pallas kernels for 11% -> 11%
where the time goes in v2:
time: 161 us
  waiting for transfers between devices  63.3 us (39%)
  starting transfers between devices  59.8 us (37%)
  Pallas kernels  25.7 us (16%)
  matrix products  6.6 us (4%)
  local copies, waits for them, and re-layouts  2.18 us (1%)
  other arithmetic  2.14 us (1%)
    ppermute x27, starting transfers between devices, send(): return lax.ppermute(x, EXPERT, self.forward)  43.8 us
    ppermute x27, waiting for transfers between devices, send(): return lax.ppermute(x, EXPERT, self.forward)  39 us
    pallas_call x17, Pallas kernels, vmem_call(): pl.pallas_call(kernel, out_shape=outs, in_specs=specs, out_specs=[pl.Bloc...  25.7 us
    ppermute x8, waiting for transfers between devices, across(): return lax.ppermute(x, DP, [(0, 1), (1, 0)])  20.9 us
    ppermute x8, starting transfers between devices, across(): return lax.ppermute(x, DP, [(0, 1), (1, 0)])  11.4 us
    dot_general x20, matrix products, project(): total = jnp.dot(act, down, preferred_element_type=F32)  6.6 us
    ppermute x33, starting transfers between devices, swap(): return lax.ppermute(x, EXPERT, self.swap_pairs)  4.59 us
    ppermute x33, waiting for transfers between devices, swap(): return lax.ppermute(x, EXPERT, self.swap_pairs)  3.36 us
  transfers between devices with their start and end apart: 68, of which 30 were waited for; matrix products, arithmetic and copies ran while one was open for 5% of the time, Pallas kernels for 11%

profile of v2, /device:TPU:0, one launch (start us, length us, event | category | flops | bytes accessed | tf_op | source)
XLA Modules:
  0.0 161.1 jit_solution(9927643689652438089)
XLA Ops:
  0.6 1.8 %shard_map.173.refs_0_.refs_10_ = bf16[136,1024]{1,0:T(8,128)(2,1)} custom-call(bf16[128,1024]{1,0:T(8,128)(2,1)} %tok_hbm.1, s32[4,128]{1,0:T(4,128)} %bitcast.86, f32[4,128]{1,0:T(4,128)} %bitcast.87), custom_call_target="tpu_custom_call" | custom-call | bytes 544768 | tf_op jit(solution)/shard_map/pallas_call | solution.py:281
  3.0 2.6 %collective-permute-start.1 = (bf16[704,512]{1,0:T(8,128)(2,1)}, bf16[704,512]{1,0:T(8,128)(2,1)S(1)}, u32[]{:S(2)}, u32[]{:S(2)}) collective-permute-start(bf16[704,512]{1,0:T(8,128)(2,1)} %bitcast.74), channel_id=1, source_target_pairs={{0,16},{16,0},{1,17},{17,1},{2,18},{18,2},{3,19},{19,3},{4,20},{20... | collective-permute-start | bytes 2162696 | tf_op jit(solution)/shard_map/ppermute | solution.py:751
  8.7 3.6 %collective-permute-done.2.refs_0_.refs_12_ = bf16[136,1024]{1,0:T(8,128)(2,1)S(1)} collective-permute-done((bf16[136,1024]{1,0:T(8,128)(2,1)}, bf16[136,1024]{1,0:T(8,128)(2,1)S(1)}, u32[]{:S(2)}, u32[]{:S(2)}) %collective-permute-start.2) | collective-permute-done | bytes 278560 | tf_op jit(solution)/shard_map/ppermute | solution.py:62
  16.9 2.0 %collective-permute-done.7.refs_0_.refs_16_ = bf16[136,1024]{1,0:T(8,128)(2,1)S(1)} collective-permute-done((bf16[136,1024]{1,0:T(8,128)(2,1)S(1)}, bf16[136,1024]{1,0:T(8,128)(2,1)S(1)}, u32[]{:S(2)}, u32[]{:S(2)}) %collective-permute-start.7) | collective-permute-done | bytes 278560 | tf_op jit(solution)/shard_map/ppermute | solution.py:62
  18.9 3.8 %collective-permute-done.1.refs_3_.refs_5_ = bf16[704,512]{1,0:T(8,128)(2,1)S(1)} collective-permute-done((bf16[704,512]{1,0:T(8,128)(2,1)}, bf16[704,512]{1,0:T(8,128)(2,1)S(1)}, u32[]{:S(2)}, u32[]{:S(2)}) %collective-permute-start.1) | collective-permute-done | bytes 720928 | tf_op jit(solution)/shard_map/ppermute | solution.py:751
  25.9 2.2 %collective-permute-start.12 = (bf16[136,1024]{1,0:T(8,128)(2,1)S(1)}, bf16[136,1024]{1,0:T(8,128)(2,1)S(1)}, u32[]{:S(2)}, u32[]{:S(2)}) collective-permute-start(bf16[136,1024]{1,0:T(8,128)(2,1)S(1)} %collective-permute-done.7.refs_0_.refs_16_), channel_id=1, source_target_pairs={{0,4},{1,3},{4,8},{5,1},{8,12},{9,5},{12,14},{13,9},{14,10},{15,13... | collective-permute-start | bytes 835592 | tf_op jit(solution)/shard_map/ppermute | solution.py:62
  37.1 2.1 %collective-permute-start.36 = (f32[1,512]{1,0:T(1,128)S(1)}, f32[1,512]{1,0:T(1,128)S(1)}, u32[]{:S(2)}, u32[]{:S(2)}) collective-permute-start(f32[1,512]{1,0:T(1,128)S(1)} %bitcast.80), channel_id=1, source_target_pairs={{0,16},{16,0},{1,17},{17,1},{2,18},{18,2},{3,19},{19,3},{4,20},{20... | collective-permute-start | bytes 6152 | tf_op jit(solution)/shard_map/ppermute | solution.py:751
  51.3 2.0 %collective-permute-done.28 = bf16[128,512]{1,0:T(8,128)(2,1)S(1)} collective-permute-done((bf16[128,512]{1,0:T(8,128)(2,1)S(1)}, bf16[128,512]{1,0:T(8,128)(2,1)S(1)}, u32[]{:S(2)}, u32[]{:S(2)}) %collective-permute-start.28) | collective-permute-done | bytes 131104 | tf_op jit(solution)/shard_map/ppermute | solution.py:62
  57.3 2.4 %collective-permute-done.21 = bf16[256,512]{1,0:T(8,128)(2,1)S(1)} collective-permute-done((bf16[256,512]{1,0:T(8,128)(2,1)S(1)}, bf16[256,512]{1,0:T(8,128)(2,1)S(1)}, u32[]{:S(2)}, u32[]{:S(2)}) %collective-permute-start.21) | collective-permute-done | bytes 262176 | tf_op jit(solution)/shard_map/ppermute | solution.py:62
  60.1 2.4 %collective-permute-done.30 = bf16[256,512]{1,0:T(8,128)(2,1)S(1)} collective-permute-done((bf16[256,512]{1,0:T(8,128)(2,1)S(1)}, bf16[256,512]{1,0:T(8,128)(2,1)S(1)}, u32[]{:S(2)}, u32[]{:S(2)}) %collective-permute-start.30) | collective-permute-done | bytes 262176 | tf_op jit(solution)/shard_map/ppermute | solution.py:62
  66.6 2.3 %collective-permute-done.22 = bf16[256,512]{1,0:T(8,128)(2,1)S(1)} collective-permute-done((bf16[256,512]{1,0:T(8,128)(2,1)S(1)}, bf16[256,512]{1,0:T(8,128)(2,1)S(1)}, u32[]{:S(2)}, u32[]{:S(2)}) %collective-permute-start.22) | collective-permute-done | bytes 262176 | tf_op jit(solution)/shard_map/ppermute | solution.py:62
  72.1 1.8 %collective-permute-start.33 = (bf16[256,512]{1,0:T(8,128)(2,1)S(1)}, bf16[256,512]{1,0:T(8,128)(2,1)S(1)}, u32[]{:S(2)}, u32[]{:S(2)}) collective-permute-start(bf16[256,512]{1,0:T(8,128)(2,1)S(1)} %fusion.9), channel_id=1, source_target_pairs={{0,4},{1,3},{4,8},{5,1},{8,12},{9,5},{12,14},{13,9},{14,10},{15,13... | collective-permute-start | bytes 786440 | tf_op jit(solution)/shard_map/ppermute | solution.py:62
  73.9 1.8 %collective-permute-done.23 = bf16[256,512]{1,0:T(8,128)(2,1)S(1)} collective-permute-done((bf16[256,512]{1,0:T(8,128)(2,1)S(1)}, bf16[256,512]{1,0:T(8,128)(2,1)S(1)}, u32[]{:S(2)}, u32[]{:S(2)}) %collective-permute-start.23) | collective-permute-done | bytes 262176 | tf_op jit(solution)/shard_map/ppermute | solution.py:62
  76.4 2.3 %collective-permute-done.33 = bf16[256,512]{1,0:T(8,128)(2,1)S(1)} collective-permute-done((bf16[256,512]{1,0:T(8,128)(2,1)S(1)}, bf16[256,512]{1,0:T(8,128)(2,1)S(1)}, u32[]{:S(2)}, u32[]{:S(2)}) %collective-permute-start.33) | collective-permute-done | bytes 262176 | tf_op jit(solution)/shard_map/ppermute | solution.py:62
  90.8 3.1 %collective-permute-done.39.refs_2_.refs_12_ = bf16[256,512]{1,0:T(8,128)(2,1)S(1)} collective-permute-done((bf16[256,512]{1,0:T(8,128)(2,1)S(1)}, bf16[256,512]{1,0:T(8,128)(2,1)S(1)}, u32[]{:S(2)}, u32[]{:S(2)}) %collective-permute-start.39) | collective-permute-done | bytes 262176 | tf_op jit(solution)/shard_map/ppermute | solution.py:62
  104.7 2.0 %collective-permute-done.48.refs_0_.refs_16_ = bf16[256,512]{1,0:T(8,128)(2,1)S(1)} collective-permute-done((bf16[256,512]{1,0:T(8,128)(2,1)S(1)}, bf16[256,512]{1,0:T(8,128)(2,1)S(1)}, u32[]{:S(2)}, u32[]{:S(2)}) %collective-permute-start.48) | collective-permute-done | bytes 262176 | tf_op jit(solution)/shard_map/ppermute | solution.py:62
  106.7 2.8 %collective-permute-done.52.refs_4_.refs_13_ = bf16[256,512]{1,0:T(8,128)(2,1)S(1)} collective-permute-done((bf16[256,512]{1,0:T(8,128)(2,1)S(1)}, bf16[256,512]{1,0:T(8,128)(2,1)S(1)}, u32[]{:S(2)}, u32[]{:S(2)}) %collective-permute-start.52) | collective-permute-done | bytes 262176 | tf_op jit(solution)/shard_map/ppermute | solution.py:62
  116.2 2.6 %shard_map.182 = (bf16[128,704]{1,0:T(8,128)(2,1)S(1)}, bf16[128,704]{1,0:T(8,128)(2,1)S(1)}, bf16[256,704]{1,0:T(8,128)(2,1)S(1)}, bf16[256,704]{1,0:T(8,128)(2...) custom-call(bf16[128,512]{1,0:T(8,128)(2,1)S(1)} %get-tuple-element.73.refs_0_.refs_10_, ...), custom_call_target="tpu_custom_call" | custom-call | flops 1845493760 | bytes 7667712 | tf_op jit(solution)/shard_map/pallas_call | solution.py:281
  118.9 1.8 %shard_map.183 = (bf16[256,704]{1,0:T(8,128)(2,1)S(1)}, bf16[256,704]{1,0:T(8,128)(2,1)S(1)}, bf16[128,704]{1,0:T(8,128)(2,1)S(1)}, bf16[128,704]{1,0:T(8,128)(2,1)S(1)}) custom-call(bf16[256,512]{1,0:T(8,128)(2,1)S(1)} %collective-permute-done.48.refs_0_.refs_16_, bf16[256,512]{1,0:T(8,128)(2,1)S(1)} %collective-permute-done.49.refs_1_.refs_17_, ...), custom_call_target="tpu_custom_call" | custom-call | flops 1107296256 | bytes 5177344 | tf_op jit(solution)/shard_map/pallas_call | solution.py:281
  131.2 3.1 %collective-permute-done.64.refs_6_ = bf16[64,1152]{1,0:T(8,128)(2,1)S(1)} collective-permute-done((bf16[64,1152]{1,0:T(8,128)(2,1)S(1)}, bf16[64,1152]{1,0:T(8,128)(2,1)S(1)}, u32[]{:S(2)}, u32[]{:S(2)}) %collective-permute-start.64) | collective-permute-done | bytes 147488 | tf_op jit(solution)/shard_map/ppermute | solution.py:62
  137.5 1.7 %shard_map.186 = bf16[704,512]{1,0:T(8,128)(2,1)S(1)} custom-call(bf16[128,704]{1,0:T(8,128)(2,1)S(1)} %get-tuple-element.53.refs_0_, bf16[128,704]{1,0:T(8,128)(2,1)S(1)} %get-tuple-element.62.refs_1_, bf16[256,704]{1,0:T(8,128)(2,1)S(1)} %get-tuple-element.65.refs_2_, bf16[256,704]{1,0:T(8,128)(2,1)S(1)} %get-tuple-element.54.refs_3_, ...), custom_call_target="tpu_custom_call" | custom-call | flops 1476395008 | bytes 5701632 | tf_op jit(solution)/shard_map/pallas_call | solution.py:281
  139.4 2.1 %collective-permute-done.56 = bf16[704,512]{1,0:T(8,128)(2,1)S(1)} collective-permute-done((bf16[704,512]{1,0:T(8,128)(2,1)S(1)}, bf16[704,512]{1,0:T(8,128)(2,1)S(1)}, u32[]{:S(2)}, u32[]{:S(2)}) %collective-permute-start.56) | collective-permute-done | bytes 720928 | tf_op jit(solution)/shard_map/ppermute | solution.py:751
  142.5 13.9 %collective-permute-done.58 = bf16[704,512]{1,0:T(8,128)(2,1)S(1)} collective-permute-done((bf16[704,512]{1,0:T(8,128)(2,1)S(1)}, bf16[704,512]{1,0:T(8,128)(2,1)S(1)}, u32[]{:S(2)}, u32[]{:S(2)}) %collective-permute-start.58) | collective-permute-done | bytes 720928 | tf_op jit(solution)/shard_map/ppermute | solution.py:751
  157.5 3.5 %shard_map.189 = (f32[512,1024]{1,0:T(8,128)}, f32[1,512]{1,0:T(1,128)}) custom-call(s32[16,16]{1,0:T(8,128)S(1)} %copy-done.13, bf16[32,1152]{1,0:T(8,128)(2,1)S(1)} %constant_dynamic-update-slice_fusion.refs_0_, bf16[32,1152]{1,0:T(8,128)(2,1)S(1)} %collective-permute-done.59.refs_1_, bf16[64,1152]{1,0:T(8,128)(2,1)S(1)} %collective-permute-done.60.refs_2_, ...), custom_call_target="tpu_custom_call" | custom-call | flops 1073741824 | bytes 4330496 | tf_op jit(solution)/shard_map/pallas_call | solution.py:281
  (187 shorter events, 90.0 us)
Async XLA Ops:
  3.0 19.8 %collective-permute-start.1 = (bf16[704,512]{1,0:T(8,128)(2,1)}, bf16[704,512]{1,0:T(8,128)(2,1)S(1)}, u32[]{:S(2)}, u32[]{:S(2)}) collective-permute-start(bf16[704,512]{1,0:T(8,128)(2,1)} %bitcast.74), channel_id=1, source_target_pairs={{0,16},{16,0},{1,17},{17,1},{2,18},{18,2},{3,19},{19,3},{4,20},{20... | collective-permute-start | bytes 2162696 | tf_op jit(solution)/shard_map/ppermute | solution.py:751
  7.1 8.2 %collective-permute-start.3 = (bf16[136,1024]{1,0:T(8,128)(2,1)S(1)}, bf16[136,1024]{1,0:T(8,128)(2,1)S(1)}, u32[]{:S(2)}, u32[]{:S(2)}) collective-permute-start(bf16[136,1024]{1,0:T(8,128)(2,1)S(1)} %collective-permute-done.refs_1_.refs_11_), channel_id=1, source_target_pairs={{0,4},{1,3},{4,8},{5,1},{8,12},{9,5},{12,14},{13,9},{14,10},{15,13... | collective-permute-start | bytes 835592 | tf_op jit(solution)/shard_map/ppermute | solution.py:62
  13.9 12.0 %collective-permute-start.4 = (bf16[136,1024]{1,0:T(8,128)(2,1)S(1)}, bf16[136,1024]{1,0:T(8,128)(2,1)S(1)}, u32[]{:S(2)}, u32[]{:S(2)}) collective-permute-start(bf16[136,1024]{1,0:T(8,128)(2,1)S(1)} %collective-permute-done.2.refs_0_.refs_12_), channel_id=1, source_target_pairs={{0,1},{1,0},{2,3},{3,2},{4,5},{5,4},{6,7},{7,6},{8,9},{9,8},{10,11... | collective-permute-start | bytes 835592 | tf_op jit(solution)/shard_map/ppermute | solution.py:65
  15.3 12.8 %collective-permute-start.8 = (bf16[136,1024]{1,0:T(8,128)(2,1)S(1)}, bf16[136,1024]{1,0:T(8,128)(2,1)S(1)}, u32[]{:S(2)}, u32[]{:S(2)}) collective-permute-start(bf16[136,1024]{1,0:T(8,128)(2,1)S(1)} %collective-permute-done.3.refs_1_.refs_13_), channel_id=1, source_target_pairs={{0,4},{1,3},{4,8},{5,1},{8,12},{9,5},{12,14},{13,9},{14,10},{15,13... | collective-permute-start | bytes 835592 | tf_op jit(solution)/shard_map/ppermute | solution.py:62
  16.9 11.4 %collective-permute-start.5 = (bf16[136,1024]{1,0:T(8,128)(2,1)S(1)}, bf16[136,1024]{1,0:T(8,128)(2,1)S(1)}, u32[]{:S(2)}, u32[]{:S(2)}) collective-permute-start(bf16[136,1024]{1,0:T(8,128)(2,1)S(1)} %collective-permute-done.3.refs_1_.refs_13_), channel_id=1, source_target_pairs={{0,1},{1,0},{2,3},{3,2},{4,5},{5,4},{6,7},{7,6},{8,9},{9,8},{10,11... | collective-permute-start | bytes 835592 | tf_op jit(solution)/shard_map/ppermute | solution.py:65
  18.8 24.2 %collective-permute-start.25 = (bf16[704,512]{1,0:T(8,128)(2,1)}, bf16[704,512]{1,0:T(8,128)(2,1)S(1)}, u32[]{:S(2)}, u32[]{:S(2)}) collective-permute-start(bf16[704,512]{1,0:T(8,128)(2,1)} %bitcast.71), channel_id=1, source_target_pairs={{0,16},{16,0},{1,17},{17,1},{2,18},{18,2},{3,19},{19,3},{4,20},{20... | collective-permute-start | bytes 2162696 | tf_op jit(solution)/shard_map/ppermute | solution.py:751
  22.7 8.6 %collective-permute-start.9 = (bf16[136,1024]{1,0:T(8,128)(2,1)S(1)}, bf16[136,1024]{1,0:T(8,128)(2,1)S(1)}, u32[]{:S(2)}, u32[]{:S(2)}) collective-permute-start(bf16[136,1024]{1,0:T(8,128)(2,1)S(1)} %collective-permute-done.7.refs_0_.refs_16_), channel_id=1, source_target_pairs={{0,1},{1,0},{2,3},{3,2},{4,5},{5,4},{6,7},{7,6},{8,9},{9,8},{10,11... | collective-permute-start | bytes 835592 | tf_op jit(solution)/shard_map/ppermute | solution.py:65
  25.9 7.0 %collective-permute-start.12 = (bf16[136,1024]{1,0:T(8,128)(2,1)S(1)}, bf16[136,1024]{1,0:T(8,128)(2,1)S(1)}, u32[]{:S(2)}, u32[]{:S(2)}) collective-permute-start(bf16[136,1024]{1,0:T(8,128)(2,1)S(1)} %collective-permute-done.7.refs_0_.refs_16_), channel_id=1, source_target_pairs={{0,4},{1,3},{4,8},{5,1},{8,12},{9,5},{12,14},{13,9},{14,10},{15,13... | collective-permute-start | bytes 835592 | tf_op jit(solution)/shard_map/ppermute | solution.py:62
  28.3 7.3 %collective-permute-start.13 = (bf16[136,1024]{1,0:T(8,128)(2,1)S(1)}, bf16[136,1024]{1,0:T(8,128)(2,1)S(1)}, u32[]{:S(2)}, u32[]{:S(2)}) collective-permute-start(bf16[136,1024]{1,0:T(8,128)(2,1)S(1)} %collective-permute-done.8.refs_1_.refs_17_), channel_id=1, source_target_pairs={{0,4},{1,3},{4,8},{5,1},{8,12},{9,5},{12,14},{13,9},{14,10},{15,13... | collective-permute-start | bytes 835592 | tf_op jit(solution)/shard_map/ppermute | solution.py:62
  31.3 48.0 %collective-permute-start.35 = (bf16[512,1024]{1,0:T(8,128)(2,1)S(1)}, bf16[512,1024]{1,0:T(8,128)(2,1)S(1)}, u32[]{:S(2)}, u32[]{:S(2)}) collective-permute-start(bf16[512,1024]{1,0:T(8,128)(2,1)S(1)} %copy-done.3), channel_id=1, source_target_pairs={{0,16},{16,0},{1,17},{17,1},{2,18},{18,2},{3,19},{19,3},{4,20},{20... | collective-permute-start | bytes 3145736 | tf_op jit(solution)/shard_map/ppermute | solution.py:751
  37.1 42.2 %collective-permute-start.36 = (f32[1,512]{1,0:T(1,128)S(1)}, f32[1,512]{1,0:T(1,128)S(1)}, u32[]{:S(2)}, u32[]{:S(2)}) collective-permute-start(f32[1,512]{1,0:T(1,128)S(1)} %bitcast.80), channel_id=1, source_target_pairs={{0,16},{16,0},{1,17},{17,1},{2,18},{18,2},{3,19},{19,3},{4,20},{20... | collective-permute-start | bytes 6152 | tf_op jit(solution)/shard_map/ppermute | solution.py:751
  39.5 27.0 %collective-permute-start.6 = (bf16[256,512]{1,0:T(8,128)(2,1)S(1)}, bf16[256,512]{1,0:T(8,128)(2,1)S(1)}, u32[]{:S(2)}, u32[]{:S(2)}) collective-permute-start(bf16[256,512]{1,0:T(8,128)(2,1)S(1)} %convolution_convert_fusion.5), channel_id=1, source_target_pairs={{0,1},{1,0},{2,3},{3,2},{4,5},{5,4},{6,7},{7,6},{8,9},{9,8},{10,11... | collective-permute-start | bytes 786440 | tf_op jit(solution)/shard_map/ppermute | solution.py:65
  64.5 7.2 %collective-permute-start.32 = (bf16[256,512]{1,0:T(8,128)(2,1)S(1)}, bf16[256,512]{1,0:T(8,128)(2,1)S(1)}, u32[]{:S(2)}, u32[]{:S(2)}) collective-permute-start(bf16[256,512]{1,0:T(8,128)(2,1)S(1)} %fusion.10), channel_id=1, source_target_pairs={{0,4},{1,3},{4,8},{5,1},{8,12},{9,5},{12,14},{13,9},{14,10},{15,13... | collective-permute-start | bytes 786440 | tf_op jit(solution)/shard_map/ppermute | solution.py:62
  89.2 7.6 %collective-permute-start.44 = (bf16[256,512]{1,0:T(8,128)(2,1)S(1)}, bf16[256,512]{1,0:T(8,128)(2,1)S(1)}, u32[]{:S(2)}, u32[]{:S(2)}) collective-permute-start(bf16[256,512]{1,0:T(8,128)(2,1)S(1)} %pad_maximum_fusion.1), channel_id=1, source_target_pairs={{0,4},{1,3},{4,8},{5,1},{8,12},{9,5},{12,14},{13,9},{14,10},{15,13... | collective-permute-start | bytes 786440 | tf_op jit(solution)/shard_map/ppermute | solution.py:62
  101.9 9.3 %collective-permute-start.40 = (bf16[256,512]{1,0:T(8,128)(2,1)S(1)}, bf16[256,512]{1,0:T(8,128)(2,1)S(1)}, u32[]{:S(2)}, u32[]{:S(2)}) collective-permute-start(bf16[256,512]{1,0:T(8,128)(2,1)S(1)} %collective-permute-done.39.refs_2_.refs_12_), channel_id=1, source_target_pairs={{0,1},{1,0},{2,3},{3,2},{4,5},{5,4},{6,7},{7,6},{8,9},{9,8},{10,11... | collective-permute-start | bytes 786440 | tf_op jit(solution)/shard_map/ppermute | solution.py:65
  101.9 10.9 %collective-permute-start.45 = (bf16[256,512]{1,0:T(8,128)(2,1)S(1)}, bf16[256,512]{1,0:T(8,128)(2,1)S(1)}, u32[]{:S(2)}, u32[]{:S(2)}) collective-permute-start(bf16[256,512]{1,0:T(8,128)(2,1)S(1)} %collective-permute-done.44.refs_8_.refs_9_), channel_id=1, source_target_pairs={{0,1},{1,0},{2,3},{3,2},{4,5},{5,4},{6,7},{7,6},{8,9},{9,8},{10,11... | collective-permute-start | bytes 786440 | tf_op jit(solution)/shard_map/ppermute | solution.py:65
  102.4 10.3 %collective-permute-start.42 = (bf16[256,512]{1,0:T(8,128)(2,1)S(1)}, bf16[256,512]{1,0:T(8,128)(2,1)S(1)}, u32[]{:S(2)}, u32[]{:S(2)}) collective-permute-start(bf16[256,512]{1,0:T(8,128)(2,1)S(1)} %collective-permute-done.41.refs_4_.refs_14_), channel_id=1, source_target_pairs={{0,1},{1,0},{2,3},{3,2},{4,5},{5,4},{6,7},{7,6},{8,9},{9,8},{10,11... | collective-permute-start | bytes 786440 | tf_op jit(solution)/shard_map/ppermute | solution.py:65
  113.3 10.6 %collective-permute-start.60 = (bf16[64,1152]{1,0:T(8,128)(2,1)S(1)}, bf16[64,1152]{1,0:T(8,128)(2,1)S(1)}, u32[]{:S(2)}, u32[]{:S(2)}) collective-permute-start(bf16[64,1152]{1,0:T(8,128)(2,1)S(1)} %pad_maximum_fusion.2), channel_id=1, source_target_pairs={{0,4},{1,3},{4,8},{5,1},{8,12},{9,5},{12,14},{13,9},{14,10},{15,13... | collective-permute-start | bytes 442376 | tf_op jit(solution)/shard_map/ppermute | solution.py:62
  122.4 19.1 %collective-permute-start.56 = (bf16[704,512]{1,0:T(8,128)(2,1)S(1)}, bf16[704,512]{1,0:T(8,128)(2,1)S(1)}, u32[]{:S(2)}, u32[]{:S(2)}) collective-permute-start(bf16[704,512]{1,0:T(8,128)(2,1)S(1)} %shard_map.185), channel_id=1, source_target_pairs={{0,16},{16,0},{1,17},{17,1},{2,18},{18,2},{3,19},{19,3},{4,20},{20... | collective-permute-start | bytes 2162696 | tf_op jit(solution)/shard_map/ppermute | solution.py:751
  127.5 29.0 %collective-permute-start.58 = (bf16[704,512]{1,0:T(8,128)(2,1)S(1)}, bf16[704,512]{1,0:T(8,128)(2,1)S(1)}, u32[]{:S(2)}, u32[]{:S(2)}) collective-permute-start(bf16[704,512]{1,0:T(8,128)(2,1)S(1)} %shard_map.188), channel_id=1, source_target_pairs={{0,16},{16,0},{1,17},{17,1},{2,18},{18,2},{3,19},{19,3},{4,20},{20... | collective-permute-start | bytes 2162696 | tf_op jit(solution)/shard_map/ppermute | solution.py:751
  130.7 26.8 %collective-permute-start.61 = (bf16[64,1152]{1,0:T(8,128)(2,1)S(1)}, bf16[64,1152]{1,0:T(8,128)(2,1)S(1)}, u32[]{:S(2)}, u32[]{:S(2)}) collective-permute-start(bf16[64,1152]{1,0:T(8,128)(2,1)S(1)} %collective-permute-done.60.refs_2_), channel_id=1, source_target_pairs={{0,1},{1,0},{2,3},{3,2},{4,5},{5,4},{6,7},{7,6},{8,9},{9,8},{10,11... | collective-permute-start | bytes 442376 | tf_op jit(solution)/shard_map/ppermute | solution.py:65
  130.7 26.8 %collective-permute-start.63 = (bf16[64,1152]{1,0:T(8,128)(2,1)S(1)}, bf16[64,1152]{1,0:T(8,128)(2,1)S(1)}, u32[]{:S(2)}, u32[]{:S(2)}) collective-permute-start(bf16[64,1152]{1,0:T(8,128)(2,1)S(1)} %collective-permute-done.62.refs_4_), channel_id=1, source_target_pairs={{0,1},{1,0},{2,3},{3,2},{4,5},{5,4},{6,7},{7,6},{8,9},{9,8},{10,11... | collective-permute-start | bytes 442376 | tf_op jit(solution)/shard_map/ppermute | solution.py:65
  139.3 18.2 %collective-permute-start.65 = (bf16[64,1152]{1,0:T(8,128)(2,1)S(1)}, bf16[64,1152]{1,0:T(8,128)(2,1)S(1)}, u32[]{:S(2)}, u32[]{:S(2)}) collective-permute-start(bf16[64,1152]{1,0:T(8,128)(2,1)S(1)} %collective-permute-done.64.refs_6_), channel_id=1, source_target_pairs={{0,1},{1,0},{2,3},{3,2},{4,5},{5,4},{6,7},{7,6},{8,9},{9,8},{10,11... | collective-permute-start | bytes 442376 | tf_op jit(solution)/shard_map/ppermute | solution.py:65
  141.5 16.1 %collective-permute-start.67 = (bf16[32,1152]{1,0:T(8,128)(2,1)S(1)}, bf16[32,1152]{1,0:T(8,128)(2,1)S(1)}, u32[]{:S(2)}, u32[]{:S(2)}) collective-permute-start(bf16[32,1152]{1,0:T(8,128)(2,1)S(1)} %collective-permute-done.66.refs_8_), channel_id=1, source_target_pairs={{0,1},{1,0},{2,3},{3,2},{4,5},{5,4},{6,7},{7,6},{8,9},{9,8},{10,11... | collective-permute-start | bytes 221192 | tf_op jit(solution)/shard_map/ppermute | solution.py:65
  (58 other events, 272.5 us)
